TPU v7x, 512 devices: a whole 4x4x16 slice. The times are simulated.
512 devices in a mesh: lat: 16 (over z_hi, y), lon: 32 (over z_lo, x, core).
Axes of the slice: x: 4, y: 4, z: 16 (z_hi: 4, z_lo: 4; z = z_hi * 4 + z_lo), core: 2. Of those that a mesh axis runs over, the one named last changes fastest.
Arguments:
- queries: float32 [64, 1024, 512], P('lat', 'lon'), may hold values from -80 to 80
- key_rows: float32 [512, 512], P(('lat', 'lon')), may hold values from -8 to 8
- value_rows: float32 [512, 512], P(('lat', 'lon')), may hold values from -6 to 6
- cotangent: float32 [64, 1024, 512], P('lat', 'lon'), may hold values from -25 to 25
- conv_taps: float32 [9, 512], replicated, may hold values from -1.75 to 1.75
Outputs:
- query_grad: float32 [64, 1024, 512], P('lat', 'lon')
- key_grad: float32 [512, 512], P(('lat', 'lon'))
- value_grad: float32 [512, 512], P(('lat', 'lon'))
- tap_update: float32 [9, 512], replicated
All inputs are finite; a program needn't handle non-finite values.
Results may differ from a plain program's by a relative error of at most 0.0003.
Values sent between devices are 32-bit elements; how exact they have to be, the bound alone decides.
A program may use at most 64 MiB of HBM per device.

v0:
```python
import jax
import jax.numpy as jnp
from jax import lax
from jax.sharding import PartitionSpec as P

HD = 64


HIGH = lax.Precision.HIGHEST
OFFSETS = ((-1, -1), (-1, 0), (-1, 1), (0, -1), (0, 0), (0, 1), (1, -1), (1, 0), (1, 1))


def joined_along(pieces, dim):
    lengths = list(pieces.shape[1:])
    lengths[dim] *= pieces.shape[0]
    return jnp.moveaxis(pieces, 0, dim).reshape(lengths)


def copy_for_each(value, axis):
    copies = jnp.broadcast_to(value, (lax.axis_size(axis), *value.shape))
    return lax.all_to_all(copies, axis, split_axis=0, concat_axis=0, tiled=True)


def gather_directly(value, axis, dim):
    return joined_along(copy_for_each(value, axis), dim)


def extended(value, sides, width):
    for axis, dim in sides:
        peers, length = (lax.axis_size(axis), value.shape[dim])
        up = [(i, (i + 1) % peers) for i in range(peers)]
        down = [(j, i) for i, j in up]
        last = lax.slice_in_dim(value, length - width, length, axis=dim)
        initial = lax.slice_in_dim(value, 0, width, axis=dim)
        before = lax.ppermute(last, axis, up)
        after = lax.ppermute(initial, axis, down)
        value = jnp.concatenate([before, value, after], axis=dim)
    return value


def cut_along(value, dim, peers):
    lengths = value.shape
    pieces = value.reshape(*lengths[:dim], peers, lengths[dim] // peers, *lengths[dim + 1 :])
    return jnp.moveaxis(pieces, dim, 0)


def summed_on_arrival(value, axis, dim):
    peers = lax.axis_size(axis)
    pieces = lax.all_to_all(cut_along(value, dim, peers), axis, 0, 0, tiled=True)
    return jnp.sum(pieces, axis=0)


def split_heads(matrix):
    return matrix.reshape(matrix.shape[0], -1, HD)


def latitude_weights(row_count, band_index, band_count):
    line_total = row_count * band_count
    centres = (jnp.arange(line_total, dtype=jnp.float32) + 0.5) * (jnp.pi / line_total)
    mean_cosine = jnp.sum(jnp.sin(centres)) / line_total
    mine = (band_index * row_count + jnp.arange(row_count, dtype=jnp.int32)).astype(jnp.float32)
    return jnp.sin((mine + 0.5) * (jnp.pi / line_total)) / mean_cosine


def close_poles(padded, row_dim, band_index, band_count):
    height = padded.shape[row_dim]
    positions = jnp.arange(height)
    outside = (positions == 0) & (band_index == 0) | (positions == height - 1) & (
        band_index == band_count - 1
    )
    shape_mask = [1] * padded.ndim
    shape_mask[row_dim] = height
    return jnp.where(outside.reshape(shape_mask), 0.0, padded)


def spread_taps(weighted, grad_padded, conv_taps):
    row_count, col_count = (weighted.shape[0], weighted.shape[1])
    result = weighted
    for tap_index, (shift_row, shift_col) in enumerate(OFFSETS):
        result = (
            result
            + conv_taps[tap_index]
            * grad_padded[
                1 - shift_row : 1 - shift_row + row_count, 1 - shift_col : 1 - shift_col + col_count
            ]
        )
    return result


def tap_terms(weighted, out_padded):
    row_count, col_count = (weighted.shape[0], weighted.shape[1])
    term_list = []
    for shift_row, shift_col in OFFSETS:
        term_list.append(
            jnp.sum(
                out_padded[
                    1 + shift_row : 1 + shift_row + row_count,
                    1 + shift_col : 1 + shift_col + col_count,
                ]
                * weighted,
                axis=(0, 1),
            )
        )
    return jnp.stack(term_list)


def group_logits(query_part, key_part):
    return jnp.einsum(
        "qhd,khd->hqk", split_heads(query_part), split_heads(key_part), precision=HIGH
    ) * HD ** (-0.5)


def body(queries, key_rows, value_rows, cotangent, conv_taps):
    row_count, col_count, channels = queries.shape
    band_count = lax.axis_size("lat")
    band_index = lax.axis_index("lat")
    weighted = cotangent * latitude_weights(row_count, band_index, band_count)[:, None, None]
    paired_rows = jnp.concatenate([key_rows, value_rows], 1)
    paired_sector = gather_directly(paired_rows, "lon", 0)
    paired_all = lax.all_gather(paired_sector, "lat", axis=0, tiled=True)
    key_all = paired_all[:, :channels]
    value_all = paired_all[:, channels:]
    token_count = row_count * col_count
    key_count = key_all.shape[0]
    query_flat = queries.reshape(token_count, channels)
    group_width = 2 * HD
    group_count = channels // group_width
    outputs = []
    peaks = []
    sums_soft = []
    for group_index in range(group_count):
        col_start = group_index * group_width
        col_stop = col_start + group_width
        logits = group_logits(query_flat[:, col_start:col_stop], key_all[:, col_start:col_stop])
        row_peak = jnp.max(logits, -1, keepdims=True)
        raised = jnp.exp(logits - row_peak)
        normaliser = jnp.sum(raised, -1, keepdims=True)
        soft_weights = raised / normaliser
        outputs.append(
            jnp.einsum(
                "hqk,khd->qhd",
                soft_weights,
                split_heads(value_all[:, col_start:col_stop]),
                precision=HIGH,
            ).reshape(token_count, group_width)
        )
        peaks.append(row_peak)
        sums_soft.append(normaliser)
    out_flat = jnp.concatenate(outputs, 1)
    out_grid = out_flat.reshape(row_count, col_count, channels)
    both_padded = close_poles(
        extended(jnp.stack([weighted, out_grid]), (("lat", 1), ("lon", 2)), 1),
        1,
        band_index,
        band_count,
    )
    grad_padded = both_padded[0]
    out_padded = both_padded[1]
    out_grad = spread_taps(weighted, grad_padded, conv_taps)
    tap_sum = lax.psum(tap_terms(weighted, out_padded), ("lat", "lon"))
    tap_update = tap_sum / jnp.sqrt(jnp.mean(tap_sum * tap_sum) + 1e-06)
    grad_flat = out_grad.reshape(token_count, channels)
    query_parts = []
    key_parts = []
    value_parts = []
    for group_index in range(group_count):
        col_start = group_index * group_width
        col_stop = col_start + group_width
        query_heads = split_heads(query_flat[:, col_start:col_stop])
        key_heads = split_heads(key_all[:, col_start:col_stop])
        logits = jnp.einsum("qhd,khd->hqk", query_heads, key_heads, precision=HIGH) * HD ** (-0.5)
        soft_weights = jnp.exp(logits - peaks[group_index]) / sums_soft[group_index]
        grad_heads = split_heads(grad_flat[:, col_start:col_stop])
        value_parts.append(
            jnp.einsum("hqk,qhd->khd", soft_weights, grad_heads, precision=HIGH).reshape(
                key_count, group_width
            )
        )
        prob_grad = jnp.einsum(
            "qhd,khd->hqk",
            grad_heads,
            split_heads(value_all[:, col_start:col_stop]),
            precision=HIGH,
        )
        row_dot = jnp.transpose(
            jnp.sum(grad_heads * split_heads(out_flat[:, col_start:col_stop]), -1)
        )[:, :, None]
        logit_grad = soft_weights * (prob_grad - row_dot)
        query_parts.append(
            (
                jnp.einsum("hqk,khd->qhd", logit_grad, key_heads, precision=HIGH) * HD ** (-0.5)
            ).reshape(token_count, group_width)
        )
        key_parts.append(
            (
                jnp.einsum("hqk,qhd->khd", logit_grad, query_heads, precision=HIGH) * HD ** (-0.5)
            ).reshape(key_count, group_width)
        )
    paired_terms = jnp.concatenate(key_parts + value_parts, 1)
    paired_band = lax.psum_scatter(paired_terms, "lat", scatter_dimension=0, tiled=True)
    paired_grad = summed_on_arrival(paired_band, "lon", 0)
    key_grad = paired_grad[:, :channels]
    value_grad = paired_grad[:, channels:]
    query_grad = jnp.concatenate(query_parts, 1).reshape(row_count, col_count, channels)
    return (query_grad, key_grad, value_grad, tap_update)


def solution(mesh):
    placed = (
        P("lat", "lon", None),
        P(("lat", "lon"), None),
        P(("lat", "lon"), None),
        P("lat", "lon", None),
        P(),
    )
    return jax.shard_map(
        body,
        mesh=mesh,
        in_specs=placed,
        out_specs=(P("lat", "lon", None), P(("lat", "lon"), None), P(("lat", "lon"), None), P()),
        check_vma=False,
    )
```

profile of v0, /device:TPU:1, one launch (start us, length us, event | category | flops | bytes accessed | tf_op | source)
XLA Modules:
  0.0 343.2 jit_solution(12765066276765064027)
XLA Ops:
  7.2 0.7 pad_maximum_fusion.13
  8.0 18.8 %all_to_all.10 = f32[32,1,1024]{2,1,0:T(1,128)} all-to-all(f32[32,1,1024]{2,1,0:T(1,128)S(1)} %broadcast_in_dim.10), channel_id=1, replica_groups=mesh['lat'=16,'lon'=32] {'lon'}, dimensions={0} | all-to-all | bytes 262144 | tf_op jit(solution)/shard_map/all_to_all | solution.py:21
  26.9 1.0 fusion.53
  27.9 0.7 copy.151
  28.6 0.7 copy.150
  29.5 0.7 sine_reduce_fusion
  30.8 1.0 fusion.50
  31.8 88.1 %all-gather.3.cloned.1.call-done = f32[512,1,1024]{2,1,0:T(1,128)} async-done(((f32[32,1,1024]{2,1,0:T(1,128)}), f32[512,1,1024]{2,1,0:T(1,128)}) %all-gather.3.cloned.1.call-update) | async-done | bytes 2097168 | tf_op jit(solution)/shard_map/all_gather | solution.py:120
  120.0 2.1 copy.158
  122.8 0.8 copy.91
  123.9 0.9 copy.83
  124.8 1.0 fusion.56
  125.9 0.5 convolution_bitcast_fusion
  126.7 1.0 fusion.58
  127.8 1.1 convolution_bitcast_fusion.2
  128.9 1.0 copy.90
  130.0 1.0 fusion.57
  131.2 0.5 convolution_bitcast_fusion.1
  131.9 1.0 fusion.59
  133.1 1.4 convolution_bitcast_fusion.3
  134.8 2.1 collective-permute-start
  136.9 9.2 %collective-permute-start.1 = (f32[2,1,32,512]{3,2,1,0:T(8,128)S(1)}, f32[2,1,32,512]{3,2,1,0:T(8,128)S(1)}, u32[]{:S(2)}, u32[]{:S(2)}) collective-permute-start(f32[2,1,32,512]{3,2,1,0:T(8,128)S(1)} %get-tuple-element.26), channel_id=1, source_target_pairs={{32,0},{64,32},{96,64},{128,96},{160,128},{192,160},{224,192},{256... | collective-permute-start | bytes 393224 | tf_op jit(solution)/shard_map/ppermute | solution.py:36
  146.1 4.7 %collective-permute-done = f32[2,1,32,512]{3,2,1,0:T(8,128)S(1)} collective-permute-done((f32[2,1,32,512]{3,2,1,0:T(8,128)S(1)}, f32[2,1,32,512]{3,2,1,0:T(8,128)S(1)}, u32[]{:S(2)}, u32[]{:S(2)}) %collective-permute-start) | collective-permute-done | bytes 131104 | tf_op jit(solution)/shard_map/ppermute | solution.py:35
  150.9 3.2 collective-permute-start.2
  154.1 2.1 collective-permute-start.3
  156.3 3.3 collective-permute-done.3
  159.9 0.3 fusion.29
  160.2 0.7 fusion.52
  160.9 1.6 copy.153
  162.4 0.9 multiply_reduce_fusion.3
  163.3 1.6 copy.155
  164.9 0.9 multiply_reduce_fusion.1
  165.8 1.6 copy.154
  167.3 0.9 multiply_reduce_fusion.2
  168.2 1.6 copy.156
  169.8 0.9 multiply_reduce_fusion
  170.8 1.6 fusion.38
  172.4 1.0 fusion
  173.4 0.7 convolution_multiply_fusion.4
  174.1 0.7 fusion.44
  174.9 1.0 fusion.2
  175.9 0.7 convolution_multiply_fusion.6
  176.6 0.7 fusion.41
  177.4 1.0 fusion.1
  178.4 0.7 convolution_multiply_fusion.5
  179.1 0.7 fusion.47
  179.9 1.0 fusion.3
  180.9 0.7 convolution_multiply_fusion.7
  181.8 1.9 copy.146
  183.8 0.3 fusion.20
  184.1 117.4 %psum.7 = f32[9,512]{1,0:T(8,128)S(1)} all-reduce(f32[9,512]{1,0:T(8,128)S(1)} %stack.47), channel_id=1, replica_groups=mesh['lat'=16,'lon'=32] {'lat','lon'}, use_global_device_ids=true, to_apply=%region_24.25 | all-reduce | flops 4608 | bytes 36864 | tf_op jit(solution)/shard_map/psum | solution.py:160
  301.5 0.6 multiply_reduce_fusion.4
  302.8 0.4 fusion.8
  303.5 0.4 fusion.10
  304.2 0.4 fusion.9
  304.9 13.6 %reduce-scatter.4.cloned.1.call-done = f32[32,1024]{1,0:T(8,128)} async-done(((f32[512,1024]{1,0:T(8,128)}), f32[32,1024]{1,0:T(8,128)}) %reduce-scatter.4.cloned.1.call-update) | async-done | bytes 131088
  318.5 1.1 copy.147
  319.6 0.8 copy.125
  320.4 6.7 %all-to-all-start.1 = ((f32[32,1,1024]{2,1,0:T(1,128)}), f32[32,1,1024]{2,1,0:T(1,128)S(1)}, u32[]{:S(2)}, u32[]{:S(2)}) async-start(f32[32,1,1024]{2,1,0:T(1,128)} %copy.125), calls=%async_computation.1 | async-start | bytes 262144 | tf_op jit(solution)/shard_map/all_to_all | solution.py:49
  327.1 0.4 fusion.11
  327.8 0.7 pad_maximum_fusion
  328.5 0.6 broadcast_divide_fusion
  329.2 6.5 %all-to-all-done.1 = f32[32,1,1024]{2,1,0:T(1,128)S(1)} async-done(((f32[32,1,1024]{2,1,0:T(1,128)}), f32[32,1,1024]{2,1,0:T(1,128)S(1)}, u32[]{:S(2)}, u32[]{:S(2)}) %all-to-all-start.1) | async-done | bytes 131104 | tf_op jit(solution)/shard_map/all_to_all | solution.py:49
  335.7 0.6 fusion.55
  (122 shorter events, 4.4 us)
Async XLA Ops:
  7.2 112.8 %all-gather.3.cloned.1.call-start = ((), (), s32[]{:S(2)}) async-start(), calls=%async_computation.3 | async-start | bytes 2228224 | tf_op jit(solution)/shard_map/all_gather | solution.py:120
  26.8 291.7 %reduce-scatter.4.cloned.1.call-start = ((), (), s32[]{:S(2)}) async-start(), calls=%async_computation.4 | async-start | bytes 2228224
  29.4 95.3 %copy-start.17 = (f32[128,128]{0,1:T(8,128)}, f32[128,128]{0,1:T(8,128)S(1)}, u32[]{:S(2)}) copy-start(f32[128,128]{0,1:T(8,128)S(1)} %copy.152) | copy-start | bytes 196612
  122.5 3.4 copy-start.1
  122.6 3.8 %copy-start.28 = (f32[512,128]{0,1:T(8,128)}, f32[512,128]{0,1:T(8,128)S(1)}, u32[]{:S(2)}) copy-start(f32[512,128]{0,1:T(8,128)S(1)} %copy.96) | copy-start | bytes 786436
  123.8 2.9 copy-start.3
  123.9 3.9 %copy-start.26 = (f32[512,128]{0,1:T(8,128)}, f32[512,128]{0,1:T(8,128)S(1)}, u32[]{:S(2)}) copy-start(f32[512,128]{0,1:T(8,128)S(1)} %copy.86) | copy-start | bytes 786436
  123.9 2.8 copy-start.15
  126.4 3.6 %copy-start.19 = (f32[128,2,64]{0,2,1:T(8,128)}, f32[128,2,64]{0,2,1:T(8,128)S(1)}, u32[]{:S(2)}) copy-start(f32[128,2,64]{0,2,1:T(8,128)S(1)} %convolution_bitcast_fusion) | copy-start | bytes 196612
  126.4 3.6 %copy-start.13 = (f32[128,128]{0,1:T(8,128)S(1)}, f32[128,128]{0,1:T(8,128)}, u32[]{:S(2)}) copy-start(f32[128,128]{0,1:T(8,128)} %copy.151) | copy-start | bytes 196612
  127.7 3.4 %copy-start.24 = (f32[512,128]{0,1:T(8,128)S(1)}, f32[512,128]{0,1:T(8,128)}, u32[]{:S(2)}) copy-start(f32[512,128]{0,1:T(8,128)} %copy.91) | copy-start | bytes 786436
  131.7 19.2 %copy-start.21 = (f32[128,2,64]{0,2,1:T(8,128)}, f32[128,2,64]{0,2,1:T(8,128)S(1)}, u32[]{:S(2)}) copy-start(f32[128,2,64]{0,2,1:T(8,128)S(1)} %convolution_bitcast_fusion.1) | copy-start | bytes 196612
  132.9 13.2 %copy-start.34 = (f32[9,512]{1,0:T(8,128)S(1)}, f32[9,512]{1,0:T(8,128)}, u32[]{:S(2)}) copy-start(f32[9,512]{1,0:T(8,128)} %param.9) | copy-start | bytes 55300
  134.5 16.3 %copy-start.22 = (f32[128,2,64]{0,2,1:T(8,128)}, f32[128,2,64]{0,2,1:T(8,128)S(1)}, u32[]{:S(2)}) copy-start(f32[128,2,64]{0,2,1:T(8,128)S(1)} %convolution_bitcast_fusion.3) | copy-start | bytes 196612
  134.8 16.0 %collective-permute-start = (f32[2,1,32,512]{3,2,1,0:T(8,128)S(1)}, f32[2,1,32,512]{3,2,1,0:T(8,128)S(1)}, u32[]{:S(2)}, u32[]{:S(2)}) collective-permute-start(f32[2,1,32,512]{3,2,1,0:T(8,128)S(1)} %get-tuple-element.25), channel_id=1, source_target_pairs={{0,32},{32,64},{64,96},{96,128},{128,160},{160,192},{192,224},{224... | collective-permute-start | bytes 393224 | tf_op jit(solution)/shard_map/ppermute | solution.py:35
  136.9 13.9 %collective-permute-start.1 = (f32[2,1,32,512]{3,2,1,0:T(8,128)S(1)}, f32[2,1,32,512]{3,2,1,0:T(8,128)S(1)}, u32[]{:S(2)}, u32[]{:S(2)}) collective-permute-start(f32[2,1,32,512]{3,2,1,0:T(8,128)S(1)} %get-tuple-element.26), channel_id=1, source_target_pairs={{32,0},{64,32},{96,64},{128,96},{160,128},{192,160},{224,192},{256... | collective-permute-start | bytes 393224 | tf_op jit(solution)/shard_map/ppermute | solution.py:36
  150.9 9.0 %copy-start = (f32[4,32,512]{2,1,0:T(8,128)S(1)}, f32[4,32,512]{2,1,0:T(8,128)}, u32[]{:S(2)}) copy-start(f32[4,32,512]{2,1,0:T(8,128)} %param.8) | copy-start | bytes 786436
  150.9 5.4 %collective-permute-start.2 = (f32[2,6,1,512]{3,2,1,0:T(1,128)S(1)}, f32[2,6,1,512]{3,2,1,0:T(1,128)S(1)}, u32[]{:S(2)}, u32[]{:S(2)}) collective-permute-start(f32[2,6,1,512]{3,2,1,0:T(1,128)S(1)} %get-tuple-element.23), channel_id=1, source_target_pairs={{0,1},{1,2},{2,3},{3,4},{4,5},{5,6},{6,7},{7,8},{8,9},{9,10},{10,1... | collective-permute-start | bytes 73736 | tf_op jit(solution)/shard_map/ppermute | solution.py:35
  154.1 5.4 %collective-permute-start.3 = (f32[2,6,1,512]{3,2,1,0:T(1,128)S(1)}, f32[2,6,1,512]{3,2,1,0:T(1,128)S(1)}, u32[]{:S(2)}, u32[]{:S(2)}) collective-permute-start(f32[2,6,1,512]{3,2,1,0:T(1,128)S(1)} %get-tuple-element.24), channel_id=1, source_target_pairs={{1,0},{2,1},{3,2},{4,3},{5,4},{6,5},{7,6},{8,7},{9,8},{10,9},{11,1... | collective-permute-start | bytes 73736 | tf_op jit(solution)/shard_map/ppermute | solution.py:36
  159.9 9.9 %copy-start.20 = (f32[128,2,64]{0,2,1:T(8,128)S(1)}, f32[128,2,64]{0,2,1:T(8,128)}, u32[]{:S(2)}) copy-start(f32[128,2,64]{0,2,1:T(8,128)} %copy-done.19) | copy-start | bytes 196612
  169.8 2.5 copy-start.29
  169.8 2.5 copy-start.33
  170.7 2.6 copy-start.18
  170.7 3.4 copy-start.32
  172.4 2.5 copy-start.27
  173.4 2.5 copy-start.7
  174.1 1.8 copy-start.16
  174.1 2.5 copy-start.31
  174.8 2.5 copy-start.25
  175.9 2.5 copy-start.9
  176.6 1.8 copy-start.14
  176.6 2.5 copy-start.30
  177.4 2.5 copy-start.23
  178.4 1.4 copy-start.11
  180.9 0.9 copy-start.5
  183.7 119.1 %copy-start.2 = (f32[512,128]{0,1:T(8,128)S(1)}, f32[512,128]{0,1:T(8,128)}, u32[]{:S(2)}) copy-start(f32[512,128]{0,1:T(8,128)} %copy-done.1) | copy-start | bytes 786436
  183.7 119.1 %copy-start.8 = (f32[2,128,512]{1,2,0:T(8,128)S(1)}, f32[2,128,512]{1,2,0:T(8,128)}, u32[]{:S(2)}) copy-start(f32[2,128,512]{1,2,0:T(8,128)} %copy-done.7) | copy-start | bytes 1572868
  183.7 119.8 %copy-start.4 = (f32[512,128]{0,1:T(8,128)S(1)}, f32[512,128]{0,1:T(8,128)}, u32[]{:S(2)}) copy-start(f32[512,128]{0,1:T(8,128)} %copy-done.3) | copy-start | bytes 786436
  183.7 119.8 %copy-start.10 = (f32[2,128,512]{1,2,0:T(8,128)S(1)}, f32[2,128,512]{1,2,0:T(8,128)}, u32[]{:S(2)}) copy-start(f32[2,128,512]{1,2,0:T(8,128)} %copy-done.9) | copy-start | bytes 1572868
  183.7 120.5 %copy-start.12 = (f32[2,128,512]{1,2,0:T(8,128)S(1)}, f32[2,128,512]{1,2,0:T(8,128)}, u32[]{:S(2)}) copy-start(f32[2,128,512]{1,2,0:T(8,128)} %copy-done.11) | copy-start | bytes 1572868
  303.4 23.7 %copy-start.6 = (f32[2,128,512]{1,2,0:T(8,128)S(1)}, f32[2,128,512]{1,2,0:T(8,128)}, u32[]{:S(2)}) copy-start(f32[2,128,512]{1,2,0:T(8,128)} %copy-done.5) | copy-start | bytes 1572868
  320.4 15.2 %all-to-all-start.1 = ((f32[32,1,1024]{2,1,0:T(1,128)}), f32[32,1,1024]{2,1,0:T(1,128)S(1)}, u32[]{:S(2)}, u32[]{:S(2)}) async-start(f32[32,1,1024]{2,1,0:T(1,128)} %copy.125), calls=%async_computation.1 | async-start | bytes 262144 | tf_op jit(solution)/shard_map/all_to_all | solution.py:49
Sparse Core Ops, SparseCore 0:
  26.9 93.0 all-gather.2
  183.8 134.6 reduce-scatter.3
where the time goes:
time: 344 us; the launch traced here: 343 us
  blocking collectives  136 us (40%)
  waiting for transfers between devices  116 us (34%)
  starting transfers between devices  23.4 us (7%)
  local copies, waits for them, and re-layouts  21.9 us (6%)
  matrix products  19.9 us (6%)
  between operations  16.2 us (5%)
  other arithmetic  9.35 us (3%)
    psum x1, blocking collectives, body(): tap_sum = lax.psum(tap_terms(weighted, out_padded), ('lat', 'lon'))  117 us
    all_gather x1, waiting for transfers between devices, body(): paired_all = lax.all_gather(paired_sector, 'lat', axis=0, tiled=True)  88.1 us
    all_to_all x1, blocking collectives, copy_for_each(): return lax.all_to_all(copies, axis, split_axis=0, concat_axis=0, tiled=True)  18.8 us
    unnamed x3, waiting for transfers between devices  13.6 us
    unnamed x88, local copies, waits for them, and re-layouts  13.2 us
    ppermute x2, starting transfers between devices, extended(): after = lax.ppermute(initial, axis, down)  11.3 us
  transfers between devices with their start and end apart: 7, of which 5 were waited for; matrix products, arithmetic and copies ran while one was open for 3% of the time, Pallas kernels for 0%

commit v1 on v0

v1 whole, which is shorter than its diff:
```python
import functools

import jax
import jax.numpy as jnp
import numpy as np
from jax import lax
from jax.experimental import pallas as pl
from jax.experimental.pallas import tpu as pltpu
from jax.sharding import PartitionSpec as P

HD = 64
NX = 4
NY = 4
ROWS = 4
COLS = 32
F32 = jnp.float32
BF16 = jnp.bfloat16
MESH = pl.DeviceIdType.MESH


def low_lanes(shape):
    return lax.broadcasted_iota(jnp.int32, shape, len(shape) - 1) < HD


def swap(value):
    return pltpu.roll(value, HD, value.ndim - 1)


def both_low(first, second):
    return jnp.where(low_lanes(first.shape), first, swap(second))


def both_high(first, second):
    return jnp.where(low_lanes(first.shape), swap(first), second)


def split2(value):
    high = value.astype(BF16)
    return high, (value - high.astype(F32)).astype(BF16)


def split3(value):
    first = value.astype(BF16)
    rest = value - first.astype(F32)
    second = rest.astype(BF16)
    return first, second, (rest - second.astype(F32)).astype(BF16)


def dot(a, b):
    return jnp.dot(a, b, preferred_element_type=F32)


def kernel(
    sizes,
    q_ref, c_ref, k_ref, v_ref, t_ref,
    dq_ref, dk_ref, dv_ref, tu_ref,
    ws, qs, wx, qx, kvs, kvx, kvy, hus, hds, hu, hd, hb,
    taps, bs, bd, rq, ro, ak, av, kt, vt, ph, plo, dh, dlo, op, dqs, dqr,
    dkvb, rsy, zs, rsz, fxs, fxr, txs, txr,
    w_s, w_r, q_s, q_r, kx_s, kx_r, z_s, z_r, y_s, y_r, h_s, h_r,
    d_s, d_r, ry_s, ry_r, rz_s, rz_r, fx_s, fx_r, tx_s, tx_r,
):
    nx, ny, nzl, nzh = sizes
    group = 2 * nx
    nz = nzl * nzh
    band_count = nzh * ny
    wide = group * COLS
    keys = ny * nz * group
    channels = group * HD
    lat = lax.axis_index("lat")
    lon = lax.axis_index("lon")
    y = lax.rem(lat, ny)
    z_hi = lax.div(lat, ny)
    z_lo = lax.div(lon, group)
    g = lax.rem(lon, group)
    z = z_hi * nzl + z_lo

    def at(z_of, y_of, g_of):
        return (lax.div(z_of, nzl) * ny + y_of, lax.rem(z_of, nzl) * group + g_of)

    def around(value, step, count):
        return lax.rem(value + step + count, count)

    x_peers = [at(z, y, around(g, e, group)) for e in range(1, group)]
    z_peers = [at(around(z, e, nz), y, g) for e in range(1, nz)]
    y_peers = [at(z, around(y, e, ny), g) for e in range(1, ny)]

    def beside(d_lat, d_lon):
        return (around(lat, d_lat, band_count), around(z_lo, d_lon, nzl) * group + g)

    h_steps = [(1, 0), (-1, 0)] + [(a, b) for a in (-1, 0, 1) for b in (1, -1)]
    h_peers = [beside(a, b) for a, b in h_steps]

    barrier = pltpu.get_barrier_semaphore()
    partners = x_peers + z_peers + y_peers + h_peers
    for peer in partners:
        pl.semaphore_signal(barrier, inc=1, device_id=peer, device_id_type=MESH)

    def send(source, target, send_sem, recv_sem, peer):
        copy = pltpu.make_async_remote_copy(
            src_ref=source, dst_ref=target, send_sem=send_sem, recv_sem=recv_sem,
            device_id=peer, device_id_type=MESH,
        )
        copy.start()
        return copy

    started = []

    for m in range(group // 2):
        cut = slice(m * 128, (m + 1) * 128)
        k_part = k_ref[:, cut]
        v_part = v_ref[:, cut]
        kvs[2 * m] = both_low(k_part, v_part)
        kvs[2 * m + 1] = both_high(k_part, v_part)
    line_total = ROWS * band_count
    centres = (np.arange(line_total) + 0.5) * np.pi / line_total
    mean_cosine = float(np.mean(np.sin(centres)))
    line = lax.broadcasted_iota(jnp.int32, (8, 128), 0) + lat * ROWS
    weight = jnp.sin((line.astype(F32) + 0.5) * (np.pi / line_total)) / mean_cosine
    for m in range(group // 2):
        cut = slice(m * 128, (m + 1) * 128)
        for r in range(2):
            upper = c_ref[r, :, cut] * weight[r : r + 1]
            lower = c_ref[r + 2, :, cut] * weight[r + 2 : r + 3]
            ws[2 * m, r] = both_low(upper, lower)
            ws[2 * m + 1, r] = both_high(upper, lower)
    for m in range(group // 2):
        cut = slice(m * 128, (m + 1) * 128)
        for r in range(2):
            upper = q_ref[r, :, cut] * (HD ** -0.5)
            lower = q_ref[r + 2, :, cut] * (HD ** -0.5)
            qs[2 * m, r] = both_low(upper, lower)
            qs[2 * m + 1, r] = both_high(upper, lower)
    own_w = pl.multiple_of(8 + COLS * g, 8)
    own_q = pl.multiple_of(COLS * g, 8)

    pl.semaphore_wait(barrier, len(partners))

    kx_copies = []
    for e, peer in enumerate(x_peers):
        to = around(g, e + 1, group)
        kx_copies.append(send(kvs.at[to], kvx.at[g], kx_s.at[e], kx_r.at[e], peer))
    w_copies = []
    for e, peer in enumerate(x_peers):
        to = around(g, e + 1, group)
        target = wx.at[pl.ds(1, 2), pl.ds(own_w, COLS), :]
        w_copies.append(send(ws.at[to], target, w_s.at[e], w_r.at[e], peer))
    q_copies = []
    for e, peer in enumerate(x_peers):
        to = around(g, e + 1, group)
        target = qx.at[:, pl.ds(own_q, COLS), :]
        q_copies.append(send(qs.at[to], target, q_s.at[e], q_r.at[e], peer))
    kvx[g] = kvs[g]
    wx[pl.ds(1, 2), pl.ds(own_w, COLS), :] = ws[g]
    qx[:, pl.ds(own_q, COLS), :] = qs[g]

    for copy in kx_copies:
        copy.wait_recv()
    kvy[y, z] = jnp.concatenate([kvx[j] for j in range(group)], 0)
    z_copies = []
    for e, peer in enumerate(z_peers):
        z_copies.append(send(kvy.at[y, z], kvy.at[y, z], z_s.at[e], z_r.at[e], peer))

    for copy in w_copies:
        copy.wait_recv()
    half = wide // 2
    hus[...] = both_high(wx[2, 8 : 8 + half], wx[2, 8 + half : 8 + wide])
    hds[...] = both_low(wx[1, 8 : 8 + half], wx[1, 8 + half : 8 + wide])
    h_copies = []
    for i, (a, b) in enumerate(h_steps):
        if b == 0:
            source, target = (hus, hu) if a == 1 else (hds, hd)
        else:
            source = wx.at[pl.ds(1, 2), pl.ds(wide if b == 1 else 8, 8), :]
            target = hb.at[i - 2]
        h_copies.append(send(source, target, h_s.at[i], h_r.at[i], h_peers[i]))

    for copy in q_copies:
        copy.wait_recv()
    for r in range(2):
        value = qx[r]
        high = value.astype(BF16).astype(F32)
        low = value - high
        rq[r] = both_low(high, low).astype(BF16)
        rq[r + 2] = both_high(high, low).astype(BF16)
        q1, q2, q3 = split3(jnp.transpose(value))
        for part in range(2):
            rows = slice(part * HD, (part + 1) * HD)
            for place, piece in enumerate((q1, q2, q1, q2, q3, q1)):
                bs[r + 2 * part, place * HD : (place + 1) * HD] = piece[rows]

    for copy in z_copies:
        copy.wait_recv()
    y_copies = []
    for e, peer in enumerate(y_peers):
        y_copies.append(send(kvy.at[y], kvy.at[y], y_s.at[e], y_r.at[e], peer))

    pair = pl.multiple_of(lax.div(g, 2) * 128, 128)
    taps[0:9] = t_ref[:, pl.ds(pair, 128)]
    taken = taps[...]
    low = low_lanes(taken.shape)
    even = jnp.where(low, taken, swap(taken))
    odd = jnp.where(low, swap(taken), taken)
    taps[...] = jnp.where(lax.rem(g, 2) == 0, even, odd)

    for copy in h_copies:
        copy.wait_recv()
    slot = {step: i - 2 for i, step in enumerate(h_steps)}
    left, right = 7, 8 + wide
    for r in range(2):
        wx[r + 1, left : left + 1] = hb[slot[0, 1], r, 7:8]
        wx[r + 1, right : right + 1] = hb[slot[0, -1], r, 0:1]
    top = jnp.where(lat > 0, 1.0, 0.0)
    bottom = jnp.where(lat < band_count - 1, 1.0, 0.0)

    def above(low_part, own):
        return jnp.where(low_lanes(own.shape), low_part * top, swap(own))

    def below(own, high_part):
        return jnp.where(low_lanes(own.shape), swap(own), high_part * bottom)

    up = hu[...]
    down = hd[...]
    wx[0, 8 : 8 + half] = above(up, wx[2, 8 : 8 + half])
    wx[0, 8 + half : 8 + wide] = above(swap(up), wx[2, 8 + half : 8 + wide])
    wx[0, left : left + 1] = above(swap(hb[slot[1, 1], 1, 7:8]), wx[2, left : left + 1])
    wx[0, right : right + 1] = above(swap(hb[slot[1, -1], 1, 0:1]), wx[2, right : right + 1])
    wx[3, 8 : 8 + half] = below(wx[1, 8 : 8 + half], swap(down))
    wx[3, 8 + half : 8 + wide] = below(wx[1, 8 + half : 8 + wide], down)
    wx[3, left : left + 1] = below(wx[1, left : left + 1], swap(hb[slot[-1, 1], 0, 7:8]))
    wx[3, right : right + 1] = below(wx[1, right : right + 1], swap(hb[slot[-1, -1], 0, 0:1]))

    for r in range(2):
        value = wx[r + 1, 8 : 8 + wide]
        for a in (-1, 0, 1):
            for b in (-1, 0, 1):
                tap = 3 * (a + 1) + (b + 1)
                value = value + taps[tap : tap + 1] * wx[r + 1 - a, 8 - b : 8 - b + wide]
        high = value.astype(BF16).astype(F32)
        low = value - high
        ro[r] = both_low(high, low).astype(BF16)
        ro[r + 2] = both_high(high, low).astype(BF16)
        o1, o2 = split2(jnp.transpose(value))
        for part in range(2):
            rows = slice(part * HD, (part + 1) * HD)
            for place, piece in enumerate((o1, o2, o1, o2)):
                bd[r + 2 * part, place * HD : (place + 1) * HD] = piece[rows]

    for copy in y_copies:
        copy.wait_recv()
    kv = kvy[...].reshape(keys, 128)
    s1 = kv.astype(BF16).astype(F32)
    rest = kv - s1
    s2 = rest.astype(BF16).astype(F32)
    s3 = rest - s2
    low = low_lanes(kv.shape)
    r1, r2, r3 = swap(s1), swap(s2), swap(s3)
    ak[:, 0:128] = jnp.where(low, s1, r1).astype(BF16)
    ak[:, 128:256] = jnp.where(low, s2, r2).astype(BF16)
    ak[:, 256:384] = jnp.where(low, s1, r3).astype(BF16)
    av[:, 0:128] = jnp.where(low, r1, s1).astype(BF16)
    av[:, 128:256] = jnp.where(low, r2, s2).astype(BF16)
    t1, t2 = split2(jnp.transpose(kv))
    kt[0:HD] = t1[0:HD]
    kt[HD : 2 * HD] = t2[0:HD]
    vt[0:HD] = t1[HD : 2 * HD]
    vt[HD : 2 * HD] = t2[HD : 2 * HD]

    out_parts = []
    query_parts = []
    for r in range(ROWS):
        logits = dot(ak[...], bs[r])
        raised = jnp.exp(logits - jnp.max(logits, 0, keepdims=True))
        soft = raised * (1.0 / jnp.sum(raised, 0, keepdims=True))
        soft_high, soft_low = split2(soft)
        ph[r] = soft_high
        plo[r] = soft_low
        both = dot(vt[...], soft_high) + dot(vt[...], soft_low)
        out_parts.append(both[0:HD] + both[HD : 2 * HD])
        prob_grad = dot(av[...], bd[r])
        row_dot = jnp.sum(soft * prob_grad, 0, keepdims=True)
        grad_high, grad_low = split2(soft * (prob_grad - row_dot))
        dh[r] = grad_high
        dlo[r] = grad_low
        both = dot(kt[...], grad_high) + dot(kt[...], grad_low)
        query_parts.append((both[0:HD] + both[HD : 2 * HD]) * (HD ** -0.5))

    for r in range(2):
        dqs[r] = jnp.transpose(jnp.concatenate([query_parts[r], query_parts[r + 2]], 0))
        op[r] = jnp.transpose(jnp.concatenate([out_parts[r], out_parts[r + 2]], 0))
    d_copies = []
    for e, peer in enumerate(x_peers):
        to = pl.multiple_of(around(g, e + 1, group) * COLS, 8)
        source = dqs.at[:, pl.ds(to, COLS), :]
        d_copies.append(send(source, dqr.at[g], d_s.at[e], d_r.at[e], peer))
    dqr[g] = dqs[:, pl.ds(own_q, COLS), :]

    sums = []
    for a in (-1, 0, 1):
        for b in (-1, 0, 1):
            total = jnp.sum(
                op[0] * wx[1 - a, 8 - b : 8 - b + wide]
                + op[1] * wx[2 - a, 8 - b : 8 - b + wide],
                0,
                keepdims=True,
            )
            sums.append(total + swap(total))
    first = jnp.concatenate(sums[0:8], 0)
    line = lax.broadcasted_iota(jnp.int32, (8, 128), 0)
    last = jnp.where(line == 0, jnp.broadcast_to(sums[8], (8, 128)), 0.0)
    tap_tile = jnp.where(low_lanes((8, 128)), first, last)

    value_terms = dot(ph[0], ro[0]) + dot(plo[0], ro[0])
    key_terms = dot(dh[0], rq[0]) + dot(dlo[0], rq[0])
    for r in range(1, ROWS):
        value_terms = value_terms + dot(ph[r], ro[r]) + dot(plo[r], ro[r])
        key_terms = key_terms + dot(dh[r], rq[r]) + dot(dlo[r], rq[r])
    terms = jnp.where(
        low_lanes(key_terms.shape), key_terms + swap(key_terms), value_terms + swap(value_terms)
    ).reshape(ny, nz, group, 128)
    for i in range(ny):
        dkvb[i, 0:nz, 0:group] = terms[i]
        dkvb[i, nz, 0:8] = tap_tile
    ry_copies = []
    for e, peer in enumerate(y_peers):
        to = around(y, e + 1, ny)
        ry_copies.append(send(dkvb.at[to], rsy.at[y], ry_s.at[e], ry_r.at[e], peer))
    rsy[y] = dkvb[y]
    for copy in ry_copies:
        copy.wait_recv()
    total = rsy[0]
    for i in range(1, ny):
        total = total + rsy[i]
    zs[:, 0] = total[0:nz]
    zs[:, 1] = jnp.broadcast_to(total[nz : nz + 1], (nz, *total.shape[1:]))
    rz_copies = []
    for e, peer in enumerate(z_peers):
        to = around(z, e + 1, nz)
        rz_copies.append(send(zs.at[to], rsz.at[z], rz_s.at[e], rz_r.at[e], peer))
    rsz[z] = zs[z]

    for copy in d_copies:
        copy.wait_recv()
    for m in range(group // 2):
        cut = slice(m * 128, (m + 1) * 128)
        for r in range(2):
            dq_ref[r, :, cut] = both_low(dqr[2 * m, r], dqr[2 * m + 1, r])
            dq_ref[r + 2, :, cut] = both_high(dqr[2 * m, r], dqr[2 * m + 1, r])

    for copy in rz_copies:
        copy.wait_recv()
    total = rsz[0]
    for i in range(1, nz):
        total = total + rsz[i]
    for j in range(group):
        fxs[j] = total[0, j : j + 1]
    txs[...] = total[1]
    fx_copies = []
    tx_copies = []
    for e, peer in enumerate(x_peers):
        to = around(g, e + 1, group)
        fx_copies.append(send(fxs.at[to], fxr.at[g], fx_s.at[e], fx_r.at[e], peer))
        tx_copies.append(send(txs, txr.at[g], tx_s.at[e], tx_r.at[e], peer))
    fxr[g] = fxs[g]
    txr[g] = txs[...]
    for copy in fx_copies + tx_copies:
        copy.wait_recv()
    for m in range(group // 2):
        cut = slice(m * 128, (m + 1) * 128)
        dk_ref[:, cut] = both_low(fxr[2 * m], fxr[2 * m + 1])
        dv_ref[:, cut] = both_high(fxr[2 * m], fxr[2 * m + 1])
    square = txr[0] * txr[0]
    for i in range(1, group):
        square = square + txr[i] * txr[i]
    mean = jnp.sum(square) * (1.0 / (9 * channels))
    scale = jnp.sqrt(jnp.full((8, 128), mean, F32) + 1e-6)
    for m in range(group // 2):
        cut = slice(m * 128, (m + 1) * 128)
        one, two = txr[2 * m, 0:8], txr[2 * m + 1, 0:8]
        tu_ref[0:8, cut] = both_low(one, two) / scale
        tu_ref[8:9, cut] = (both_high(one, two) / scale)[0:1]

    for copies in (
        kx_copies, w_copies, q_copies, z_copies, h_copies, y_copies,
        d_copies, ry_copies, rz_copies, fx_copies, tx_copies,
    ):
        for copy in copies:
            copy.wait_send()


def body(sizes, queries, key_rows, value_rows, cotangent, conv_taps):
    nx, ny, nzl, nzh = sizes
    group = 2 * nx
    nz = nzl * nzh
    wide = group * COLS
    keys = ny * nz * group
    tile = max(group, 8)
    channels = group * HD
    vmem = pltpu.VMEM
    scratch = [
        vmem((group, 2, COLS, 128), F32),
        vmem((group, 2, COLS, 128), F32),
        vmem((4, wide + 16, 128), F32),
        vmem((2, wide, 128), F32),
        vmem((group, 1, 128), F32),
        vmem((group, 1, 128), F32),
        vmem((ny, nz, group, 128), F32),
        vmem((wide // 2, 128), F32),
        vmem((wide // 2, 128), F32),
        vmem((wide // 2, 128), F32),
        vmem((wide // 2, 128), F32),
        vmem((6, 2, 8, 128), F32),
        vmem((16, 128), F32),
        vmem((ROWS, 6 * HD, wide), BF16),
        vmem((ROWS, 4 * HD, wide), BF16),
        vmem((ROWS, wide, 128), BF16),
        vmem((ROWS, wide, 128), BF16),
        vmem((keys, 6 * HD), BF16),
        vmem((keys, 4 * HD), BF16),
        vmem((128, keys), BF16),
        vmem((128, keys), BF16),
        vmem((ROWS, keys, wide), BF16),
        vmem((ROWS, keys, wide), BF16),
        vmem((ROWS, keys, wide), BF16),
        vmem((ROWS, keys, wide), BF16),
        vmem((2, wide, 128), F32),
        vmem((2, wide, 128), F32),
        vmem((group, 2, COLS, 128), F32),
        vmem((ny, nz + 1, tile, 128), F32),
        vmem((ny, nz + 1, tile, 128), F32),
        vmem((nz, 2, tile, 128), F32),
        vmem((nz, 2, tile, 128), F32),
        vmem((group, 1, 128), F32),
        vmem((group, 1, 128), F32),
        vmem((tile, 128), F32),
        vmem((group, tile, 128), F32),
    ]
    counts = (
        group - 1, group - 1, group - 1, nz - 1, ny - 1, 8,
        group - 1, ny - 1, nz - 1, group - 1, group - 1,
    )
    for count in counts:
        scratch += [pltpu.SemaphoreType.DMA((count,)), pltpu.SemaphoreType.DMA((count,))]
    whole = pl.BlockSpec(memory_space=pltpu.VMEM)
    return pl.pallas_call(
        functools.partial(kernel, sizes),
        out_shape=(
            jax.ShapeDtypeStruct((ROWS, COLS, channels), F32),
            jax.ShapeDtypeStruct((1, channels), F32),
            jax.ShapeDtypeStruct((1, channels), F32),
            jax.ShapeDtypeStruct((9, channels), F32),
        ),
        in_specs=[whole] * 5,
        out_specs=(whole,) * 4,
        scratch_shapes=scratch,
        compiler_params=pltpu.CompilerParams(
            collective_id=0, has_side_effects=True, vmem_limit_bytes=48 << 20
        ),
    )(queries, cotangent, key_rows, value_rows, conv_taps)


def solution(mesh):
    sizes = (NX, NY, mesh.shape["lon"] // (2 * NX), mesh.shape["lat"] // NY)
    placed = (
        P("lat", "lon", None),
        P(("lat", "lon"), None),
        P(("lat", "lon"), None),
        P("lat", "lon", None),
        P(),
    )
    return jax.shard_map(
        functools.partial(body, sizes),
        mesh=mesh,
        in_specs=placed,
        out_specs=(P("lat", "lon", None), P(("lat", "lon"), None), P(("lat", "lon"), None), P()),
        check_vma=False,
    )
```

time: 344 us -> 69.5 us (0.20)
  blocking collectives: 136 us -> 0 us
  waiting for transfers between devices: 116 us -> 0 us
  Pallas kernels: 0 us -> 62.1 us
  starting transfers between devices: 23.4 us -> 0 us
  matrix products: 19.9 us -> 0 us
  between operations: 16.2 us -> 0.65 us
  local copies, waits for them, and re-layouts: 21.9 us -> 6.49 us
  other arithmetic: 9.35 us -> 0 us
    psum x1 -> x0, blocking collectives: 117 us -> none  [body(): tap_sum = lax.psum(tap_terms(weighted, out_padded), ('lat', 'lon'))]
    all_gather x1 -> x0, waiting for transfers between devices: 88.1 us -> none  [body(): paired_all = lax.all_gather(paired_sector, 'lat', axis=0, tiled=True)]
    pallas_call x0 -> x1, Pallas kernels: none -> 62.1 us  [body(): pl.pallas_call(functools.partial(kernel, sizes), out_shape=(jax.ShapeDtyp...]
    dot_general x24 -> x0, matrix products: 19.9 us -> none  [the longest x4 4.05 us: body(): jnp.einsum('qhd,khd->hqk', grad_heads, split_heads(value_all[:, col_start...]
    all_to_all x1 -> x0, blocking collectives: 18.8 us -> none  [copy_for_each(): return lax.all_to_all(copies, axis, split_axis=0, concat_axis=0, tiled=True)]
    ppermute x4 -> x0, starting transfers between devices: 16.6 us -> none  [the longest x2 11.3 us: extended(): after = lax.ppermute(initial, axis, down)]
    unnamed x3 -> x0, waiting for transfers between devices: 13.6 us -> none
    ppermute x4 -> x0, waiting for transfers between devices: 7.99 us -> none  [the longest x2 4.69 us: extended(): before = lax.ppermute(last, axis, up)]
  transfers between devices with their start and end apart: 7 -> 0, of which waited for: 5 -> 0; matrix products, arithmetic and copies ran while one was open for 3% -> 0% of each run, Pallas kernels for 0% -> 0%
where the time goes in v1:
time: 69.5 us; the launch traced here: 69.2 us
  Pallas kernels  62.1 us (89%)
  local copies, waits for them, and re-layouts  6.49 us (9%)
    pallas_call x1, Pallas kernels, body(): pl.pallas_call(functools.partial(kernel, sizes), out_shape=(jax.ShapeDtyp...  62.1 us
    unnamed x14, local copies, waits for them, and re-layouts  6.49 us

profile of v1, /device:TPU:1, one launch (start us, length us, event | category | flops | bytes accessed | tf_op | source)
XLA Modules:
  0.0 69.2 jit_solution(17117759454149642089)
XLA Ops:
  0.6 0.0 copy-start
  0.6 0.9 %copy-done = f32[4,32,512]{2,1,0:T(8,128)S(1)} copy-done((f32[4,32,512]{2,1,0:T(8,128)S(1)}, f32[4,32,512]{2,1,0:T(8,128)}, u32[]{:S(2)}) %copy-start) | copy-done | bytes 262168
  1.6 0.0 copy-start.1
  1.6 0.9 %copy-done.1 = f32[4,32,512]{2,1,0:T(8,128)S(1)} copy-done((f32[4,32,512]{2,1,0:T(8,128)S(1)}, f32[4,32,512]{2,1,0:T(8,128)}, u32[]{:S(2)}) %copy-start.1) | copy-done | bytes 262168
  2.5 0.0 copy-start.2
  2.5 0.8 %copy-done.2 = f32[9,512]{1,0:T(8,128)S(1)} copy-done((f32[9,512]{1,0:T(8,128)S(1)}, f32[9,512]{1,0:T(8,128)}, u32[]{:S(2)}) %copy-start.2) | copy-done | bytes 18456
  3.3 0.0 copy-start.3
  3.3 0.7 copy-done.3
  4.0 0.0 copy-start.4
  4.0 0.7 copy-done.4
  4.7 62.1 %shard_map.84 = (f32[4,32,512]{2,1,0:T(8,128)S(1)}, f32[1,512]{1,0:T(1,128)S(1)}, f32[1,512]{1,0:T(1,128)S(1)}, f32[9,512]{1,0:T(8,128)S(1)}) custom-call(f32[4,32,512]{2,1,0:T(8,128)S(1)} %copy-done, f32[4,32,512]{2,1,0:T(8,128)S(1)} %copy-done.1, f32[1,512]{1,0:T(1,128)S(1)} %copy-done.3, f32[1,512]{1,0:T(1,128)S(1)} %copy-done.4, f32[9,512]{1,0:T(8,128)S(1)} %copy-done.2), custom_call_target="tpu_custom_call" | custom-call | tf_op jit(solution)/shard_map/pallas_call | solution.py:445
  66.8 0.7 %copy.13 = f32[4,32,512]{2,1,0:T(8,128)} copy(f32[4,32,512]{2,1,0:T(8,128)S(1)} %get-tuple-element.8) | data formatting | bytes 524288
  67.5 0.6 copy.14
  68.1 0.6 copy.15
  68.6 0.6 copy.16
Async XLA Ops:
  0.6 1.0 %copy-start = (f32[4,32,512]{2,1,0:T(8,128)S(1)}, f32[4,32,512]{2,1,0:T(8,128)}, u32[]{:S(2)}) copy-start(f32[4,32,512]{2,1,0:T(8,128)} %q_ref.1) | copy-start | bytes 786436
  1.6 0.9 %copy-start.1 = (f32[4,32,512]{2,1,0:T(8,128)S(1)}, f32[4,32,512]{2,1,0:T(8,128)}, u32[]{:S(2)}) copy-start(f32[4,32,512]{2,1,0:T(8,128)} %c_ref.1) | copy-start | bytes 786436
  2.5 0.8 %copy-start.2 = (f32[9,512]{1,0:T(8,128)S(1)}, f32[9,512]{1,0:T(8,128)}, u32[]{:S(2)}) copy-start(f32[9,512]{1,0:T(8,128)} %t_ref.1) | copy-start | bytes 55300
  3.3 0.7 copy-start.3
  4.0 0.7 copy-start.4

commit v2 on v1

v2 whole, which is shorter than its diff:
```python
import functools

import jax
import jax.numpy as jnp
import numpy as np
from jax import lax
from jax.experimental import pallas as pl
from jax.experimental.pallas import tpu as pltpu
from jax.sharding import PartitionSpec as P

HD = 64
NX = 4
NY = 4
ROWS = 4
COLS = 32
F32 = jnp.float32
BF16 = jnp.bfloat16
MESH = pl.DeviceIdType.MESH


def low_lanes(shape):
    return lax.broadcasted_iota(jnp.int32, shape, len(shape) - 1) < HD


def swap(value):
    return pltpu.roll(value, HD, value.ndim - 1)


def both_low(first, second):
    return jnp.where(low_lanes(first.shape), first, swap(second))


def both_high(first, second):
    return jnp.where(low_lanes(first.shape), swap(first), second)


def split2(value):
    high = value.astype(BF16)
    return high, (value - high.astype(F32)).astype(BF16)


def split3(value):
    first = value.astype(BF16)
    rest = value - first.astype(F32)
    second = rest.astype(BF16)
    return first, second, (rest - second.astype(F32)).astype(BF16)


def dot(a, b):
    return jnp.dot(a, b, preferred_element_type=F32)


def kernel(
    sizes,
    q_hbm, c_hbm, k_hbm, v_hbm, t_hbm,
    dq_ref, dk_ref, dv_ref, tu_ref,
    q_ref, c_ref, k_ref, v_ref, t_ref, in_s,
    ws, qs, wx, qx, kvs, kvx, kvy, hus, hds, hu, hd, hb,
    taps, bs, bd, rq, ro, ak, av, kt, vt, pf, ph, plo, dh, dlo, op, dqs, dqr,
    dkvb, rsy, zs, rsz, fxs, fxr, txs, txr, tys, tyr, tzs, tzr,
    w_s, w_r, q_s, q_r, kx_s, kx_r, z_s, z_r, y_s, y_r, h_s, h_r,
    d_s, d_r, ry_s, ry_r, rz_s, rz_r, fx_s, fx_r, tx_s, tx_r, ty_s, ty_r, tz_s, tz_r,
):
    nx, ny, nzl, nzh = sizes
    group = 2 * nx
    nz = nzl * nzh
    band_count = nzh * ny
    wide = group * COLS
    keys = ny * nz * group
    channels = group * HD
    lat = lax.axis_index("lat")
    lon = lax.axis_index("lon")
    y = lax.rem(lat, ny)
    z_hi = lax.div(lat, ny)
    z_lo = lax.div(lon, group)
    g = lax.rem(lon, group)
    z = z_hi * nzl + z_lo

    def at(z_of, y_of, g_of):
        return (lax.div(z_of, nzl) * ny + y_of, lax.rem(z_of, nzl) * group + g_of)

    def around(value, step, count):
        return lax.rem(value + step + count, count)

    x_peers = [at(z, y, around(g, e, group)) for e in range(1, group)]
    z_steps = sorted(range(1, nz), key=lambda e: -min(e, nz - e))
    z_peers = [at(around(z, e, nz), y, g) for e in z_steps]
    y_peers = [at(z, around(y, e, ny), g) for e in range(1, ny)]

    def beside(d_lat, d_lon):
        return (around(lat, d_lat, band_count), around(z_lo, d_lon, nzl) * group + g)

    h_steps = [(1, 0), (-1, 0)] + [(a, b) for a in (-1, 0, 1) for b in (1, -1)]
    h_peers = [beside(a, b) for a, b in h_steps]

    barrier = pltpu.get_barrier_semaphore()
    inputs = []
    for i, (source, target) in enumerate(
        ((k_hbm, k_ref), (v_hbm, v_ref), (c_hbm, c_ref), (q_hbm, q_ref), (t_hbm, t_ref))
    ):
        inputs.append(pltpu.make_async_copy(source, target, in_s.at[i]))
        inputs[i].start()
    partners = x_peers + z_peers + y_peers + h_peers
    for peer in partners:
        pl.semaphore_signal(barrier, inc=1, device_id=peer, device_id_type=MESH)

    def send(source, target, send_sem, recv_sem, peer):
        copy = pltpu.make_async_remote_copy(
            src_ref=source, dst_ref=target, send_sem=send_sem, recv_sem=recv_sem,
            device_id=peer, device_id_type=MESH,
        )
        copy.start()
        started.append(copy)
        return copy

    started = []
    arrived = []

    def arrive(copies):
        for copy in copies:
            copy.wait_recv()
            arrived.append(copy)

    inputs[0].wait()
    inputs[1].wait()
    for m in range(group // 2):
        cut = slice(m * 128, (m + 1) * 128)
        k_part = k_ref[:, cut]
        v_part = v_ref[:, cut]
        kvs[2 * m] = both_low(k_part, v_part)
        kvs[2 * m + 1] = both_high(k_part, v_part)
    own_w = pl.multiple_of(8 + COLS * g, 8)
    own_q = pl.multiple_of(COLS * g, 8)

    pl.semaphore_wait(barrier, len(partners))

    kx_copies = []
    for e, peer in enumerate(x_peers):
        to = around(g, e + 1, group)
        kx_copies.append(send(kvs.at[to], kvx.at[g], kx_s.at[e], kx_r.at[e], peer))
    kvx[g] = kvs[g]
    inputs[2].wait()
    line_total = ROWS * band_count
    centres = (np.arange(line_total) + 0.5) * np.pi / line_total
    mean_cosine = float(np.mean(np.sin(centres)))
    line = lax.broadcasted_iota(jnp.int32, (8, 128), 0) + lat * ROWS
    weight = jnp.sin((line.astype(F32) + 0.5) * (np.pi / line_total)) / mean_cosine
    for m in range(group // 2):
        cut = slice(m * 128, (m + 1) * 128)
        for r in range(2):
            upper = c_ref[r, :, cut] * weight[r : r + 1]
            lower = c_ref[r + 2, :, cut] * weight[r + 2 : r + 3]
            ws[2 * m, r] = both_low(upper, lower)
            ws[2 * m + 1, r] = both_high(upper, lower)
    w_copies = []
    for e, peer in enumerate(x_peers):
        to = around(g, e + 1, group)
        target = wx.at[pl.ds(1, 2), pl.ds(own_w, COLS), :]
        w_copies.append(send(ws.at[to], target, w_s.at[e], w_r.at[e], peer))
    wx[pl.ds(1, 2), pl.ds(own_w, COLS), :] = ws[g]
    inputs[3].wait()
    for m in range(group // 2):
        cut = slice(m * 128, (m + 1) * 128)
        for r in range(2):
            upper = q_ref[r, :, cut] * (HD ** -0.5)
            lower = q_ref[r + 2, :, cut] * (HD ** -0.5)
            qs[2 * m, r] = both_low(upper, lower)
            qs[2 * m + 1, r] = both_high(upper, lower)
    q_copies = []
    for e, peer in enumerate(x_peers):
        to = around(g, e + 1, group)
        target = qx.at[:, pl.ds(own_q, COLS), :]
        q_copies.append(send(qs.at[to], target, q_s.at[e], q_r.at[e], peer))
    qx[:, pl.ds(own_q, COLS), :] = qs[g]

    arrive(kx_copies)
    kvy[y, z] = jnp.concatenate([kvx[j] for j in range(group)], 0)
    z_copies = []
    for e, peer in enumerate(z_peers):
        z_copies.append(send(kvy.at[y, z], kvy.at[y, z], z_s.at[e], z_r.at[e], peer))

    arrive(w_copies)
    half = wide // 2
    hus[...] = both_high(wx[2, 8 : 8 + half], wx[2, 8 + half : 8 + wide])
    hds[...] = both_low(wx[1, 8 : 8 + half], wx[1, 8 + half : 8 + wide])
    h_copies = []
    for i, (a, b) in enumerate(h_steps):
        if b == 0:
            source, target = (hus, hu) if a == 1 else (hds, hd)
        else:
            source = wx.at[pl.ds(1, 2), pl.ds(wide if b == 1 else 8, 8), :]
            target = hb.at[i - 2]
        h_copies.append(send(source, target, h_s.at[i], h_r.at[i], h_peers[i]))

    arrive(q_copies)
    for r in range(2):
        value = qx[r]
        high = value.astype(BF16).astype(F32)
        low = value - high
        rq[r] = both_low(high, low).astype(BF16)
        rq[r + 2] = both_high(high, low).astype(BF16)
        q1, q2, q3 = split3(jnp.transpose(value))
        for part in range(2):
            rows = slice(part * HD, (part + 1) * HD)
            for place, piece in enumerate((q1, q2, q1, q2, q3, q1)):
                bs[r + 2 * part, place * HD : (place + 1) * HD] = piece[rows]

    arrive(z_copies)
    y_copies = []
    for e, peer in enumerate(y_peers):
        y_copies.append(send(kvy.at[y], kvy.at[y], y_s.at[e], y_r.at[e], peer))

    pair = pl.multiple_of(lax.div(g, 2) * 128, 128)
    inputs[4].wait()
    taps[0:9] = t_ref[:, pl.ds(pair, 128)]
    taken = taps[...]
    low = low_lanes(taken.shape)
    even = jnp.where(low, taken, swap(taken))
    odd = jnp.where(low, swap(taken), taken)
    taps[...] = jnp.where(lax.rem(g, 2) == 0, even, odd)

    arrive(y_copies)
    kv = kvy[...].reshape(keys, 128)
    s1 = kv.astype(BF16).astype(F32)
    rest = kv - s1
    s2 = rest.astype(BF16).astype(F32)
    s3 = rest - s2
    low = low_lanes(kv.shape)
    r1, r2, r3 = swap(s1), swap(s2), swap(s3)
    ak[:, 0:128] = jnp.where(low, s1, r1).astype(BF16)
    ak[:, 128:256] = jnp.where(low, s2, r2).astype(BF16)
    ak[:, 256:384] = jnp.where(low, s1, r3).astype(BF16)
    av[:, 0:128] = jnp.where(low, r1, s1).astype(BF16)
    av[:, 128:256] = jnp.where(low, r2, s2).astype(BF16)
    t1, t2 = split2(jnp.transpose(kv))
    kt[0:HD] = t1[0:HD]
    kt[HD : 2 * HD] = t2[0:HD]
    vt[0:HD] = t1[HD : 2 * HD]
    vt[HD : 2 * HD] = t2[HD : 2 * HD]

    out_parts = []
    for r in range(ROWS):
        logits = dot(ak[...], bs[r])
        raised = jnp.exp(logits - jnp.max(logits, 0, keepdims=True))
        soft = raised * (1.0 / jnp.sum(raised, 0, keepdims=True))
        soft_high, soft_low = split2(soft)
        pf[r] = soft
        ph[r] = soft_high
        plo[r] = soft_low
        both = dot(vt[...], soft_high) + dot(vt[...], soft_low)
        out_parts.append(both[0:HD] + both[HD : 2 * HD])
    for r in range(2):
        op[r] = jnp.transpose(jnp.concatenate([out_parts[r], out_parts[r + 2]], 0))

    arrive(h_copies)
    slot = {step: i - 2 for i, step in enumerate(h_steps)}
    left, right = 7, 8 + wide
    for r in range(2):
        wx[r + 1, left : left + 1] = hb[slot[0, 1], r, 7:8]
        wx[r + 1, right : right + 1] = hb[slot[0, -1], r, 0:1]
    top = jnp.where(lat > 0, 1.0, 0.0)
    bottom = jnp.where(lat < band_count - 1, 1.0, 0.0)

    def above(low_part, own):
        return jnp.where(low_lanes(own.shape), low_part * top, swap(own))

    def below(own, high_part):
        return jnp.where(low_lanes(own.shape), swap(own), high_part * bottom)

    up = hu[...]
    down = hd[...]
    wx[0, 8 : 8 + half] = above(up, wx[2, 8 : 8 + half])
    wx[0, 8 + half : 8 + wide] = above(swap(up), wx[2, 8 + half : 8 + wide])
    wx[0, left : left + 1] = above(swap(hb[slot[1, 1], 1, 7:8]), wx[2, left : left + 1])
    wx[0, right : right + 1] = above(swap(hb[slot[1, -1], 1, 0:1]), wx[2, right : right + 1])
    wx[3, 8 : 8 + half] = below(wx[1, 8 : 8 + half], swap(down))
    wx[3, 8 + half : 8 + wide] = below(wx[1, 8 + half : 8 + wide], down)
    wx[3, left : left + 1] = below(wx[1, left : left + 1], swap(hb[slot[-1, 1], 0, 7:8]))
    wx[3, right : right + 1] = below(wx[1, right : right + 1], swap(hb[slot[-1, -1], 0, 0:1]))

    for r in range(2):
        value = wx[r + 1, 8 : 8 + wide]
        for a in (-1, 0, 1):
            for b in (-1, 0, 1):
                tap = 3 * (a + 1) + (b + 1)
                value = value + taps[tap : tap + 1] * wx[r + 1 - a, 8 - b : 8 - b + wide]
        high = value.astype(BF16).astype(F32)
        low = value - high
        ro[r] = both_low(high, low).astype(BF16)
        ro[r + 2] = both_high(high, low).astype(BF16)
        o1, o2 = split2(jnp.transpose(value))
        for part in range(2):
            rows = slice(part * HD, (part + 1) * HD)
            for place, piece in enumerate((o1, o2, o1, o2)):
                bd[r + 2 * part, place * HD : (place + 1) * HD] = piece[rows]

    sums = []
    for a in (-1, 0, 1):
        for b in (-1, 0, 1):
            total = jnp.sum(
                op[0] * wx[1 - a, 8 - b : 8 - b + wide]
                + op[1] * wx[2 - a, 8 - b : 8 - b + wide],
                0,
                keepdims=True,
            )
            sums.append(total + swap(total))
    first = jnp.concatenate(sums[0:8], 0)
    line = lax.broadcasted_iota(jnp.int32, (8, 128), 0)
    last = jnp.where(line == 0, jnp.broadcast_to(sums[8], (8, 128)), 0.0)
    tap_tile = jnp.where(low_lanes((8, 128)), first, last)

    tys[...] = tap_tile
    ty_copies = []
    for e, peer in enumerate(y_peers):
        ty_copies.append(send(tys, tyr.at[y], ty_s.at[e], ty_r.at[e], peer))
    tyr[y] = tap_tile

    query_parts = []
    for r in range(ROWS):
        soft = pf[r]
        prob_grad = dot(av[...], bd[r])
        row_dot = jnp.sum(soft * prob_grad, 0, keepdims=True)
        grad_high, grad_low = split2(soft * (prob_grad - row_dot))
        dh[r] = grad_high
        dlo[r] = grad_low
        both = dot(kt[...], grad_high) + dot(kt[...], grad_low)
        query_parts.append((both[0:HD] + both[HD : 2 * HD]) * (HD ** -0.5))

    for r in range(2):
        dqs[r] = jnp.transpose(jnp.concatenate([query_parts[r], query_parts[r + 2]], 0))
    d_copies = []
    for e, peer in enumerate(x_peers):
        to = pl.multiple_of(around(g, e + 1, group) * COLS, 8)
        source = dqs.at[:, pl.ds(to, COLS), :]
        d_copies.append(send(source, dqr.at[g], d_s.at[e], d_r.at[e], peer))
    dqr[g] = dqs[:, pl.ds(own_q, COLS), :]

    arrive(ty_copies)
    total = tyr[0]
    for i in range(1, ny):
        total = total + tyr[i]
    tzs[...] = total
    tz_copies = []
    for e, peer in enumerate(z_peers):
        tz_copies.append(send(tzs, tzr.at[z], tz_s.at[e], tz_r.at[e], peer))
    tzr[z] = total

    value_terms = dot(ph[0], ro[0]) + dot(plo[0], ro[0])
    key_terms = dot(dh[0], rq[0]) + dot(dlo[0], rq[0])
    for r in range(1, ROWS):
        value_terms = value_terms + dot(ph[r], ro[r]) + dot(plo[r], ro[r])
        key_terms = key_terms + dot(dh[r], rq[r]) + dot(dlo[r], rq[r])
    terms = jnp.where(
        low_lanes(key_terms.shape), key_terms + swap(key_terms), value_terms + swap(value_terms)
    ).reshape(ny, nz, group, 128)
    for i in range(ny):
        dkvb[i] = terms[i]
    ry_copies = []
    for e, peer in enumerate(y_peers):
        to = around(y, e + 1, ny)
        ry_copies.append(send(dkvb.at[to], rsy.at[y], ry_s.at[e], ry_r.at[e], peer))
    rsy[y] = dkvb[y]
    arrive(ry_copies)
    total = rsy[0]
    for i in range(1, ny):
        total = total + rsy[i]
    zs[...] = total
    rz_copies = []
    for e, peer in enumerate(z_peers):
        to = around(z, z_steps[e], nz)
        rz_copies.append(send(zs.at[to], rsz.at[z], rz_s.at[e], rz_r.at[e], peer))
    rsz[z] = zs[z]

    arrive(tz_copies)
    total = tzr[0]
    for i in range(1, nz):
        total = total + tzr[i]
    txs[...] = total
    tx_copies = []
    for e, peer in enumerate(x_peers):
        tx_copies.append(send(txs, txr.at[g], tx_s.at[e], tx_r.at[e], peer))
    txr[g] = total

    arrive(d_copies)
    for m in range(group // 2):
        cut = slice(m * 128, (m + 1) * 128)
        for r in range(2):
            dq_ref[r, :, cut] = both_low(dqr[2 * m, r], dqr[2 * m + 1, r])
            dq_ref[r + 2, :, cut] = both_high(dqr[2 * m, r], dqr[2 * m + 1, r])

    arrive(rz_copies)
    total = rsz[0]
    for i in range(1, nz):
        total = total + rsz[i]
    for j in range(group):
        fxs[j] = total[j : j + 1]
    fx_copies = []
    for e, peer in enumerate(x_peers):
        to = around(g, e + 1, group)
        fx_copies.append(send(fxs.at[to], fxr.at[g], fx_s.at[e], fx_r.at[e], peer))
    fxr[g] = fxs[g]

    arrive(tx_copies)
    square = txr[0] * txr[0]
    for i in range(1, group):
        square = square + txr[i] * txr[i]
    mean = jnp.sum(square) * (1.0 / (9 * channels))
    scale = jnp.sqrt(jnp.full((8, 128), mean, F32) + 1e-6)
    for m in range(group // 2):
        cut = slice(m * 128, (m + 1) * 128)
        one, two = txr[2 * m, 0:8], txr[2 * m + 1, 0:8]
        tu_ref[0:8, cut] = both_low(one, two) / scale
        tu_ref[8:9, cut] = (both_high(one, two) / scale)[0:1]

    arrive(fx_copies)
    for m in range(group // 2):
        cut = slice(m * 128, (m + 1) * 128)
        dk_ref[:, cut] = both_low(fxr[2 * m], fxr[2 * m + 1])
        dv_ref[:, cut] = both_high(fxr[2 * m], fxr[2 * m + 1])
    for copy in started:
        copy.wait_send()


def body(sizes, queries, key_rows, value_rows, cotangent, conv_taps):
    nx, ny, nzl, nzh = sizes
    group = 2 * nx
    nz = nzl * nzh
    wide = group * COLS
    keys = ny * nz * group
    channels = group * HD
    vmem = pltpu.VMEM
    scratch = [
        vmem((ROWS, COLS, channels), F32),
        vmem((ROWS, COLS, channels), F32),
        vmem((1, channels), F32),
        vmem((1, channels), F32),
        vmem((9, channels), F32),
        pltpu.SemaphoreType.DMA((5,)),
        vmem((group, 2, COLS, 128), F32),
        vmem((group, 2, COLS, 128), F32),
        vmem((4, wide + 16, 128), F32),
        vmem((2, wide, 128), F32),
        vmem((group, 1, 128), F32),
        vmem((group, 1, 128), F32),
        vmem((ny, nz, group, 128), F32),
        vmem((wide // 2, 128), F32),
        vmem((wide // 2, 128), F32),
        vmem((wide // 2, 128), F32),
        vmem((wide // 2, 128), F32),
        vmem((6, 2, 8, 128), F32),
        vmem((16, 128), F32),
        vmem((ROWS, 6 * HD, wide), BF16),
        vmem((ROWS, 4 * HD, wide), BF16),
        vmem((ROWS, wide, 128), BF16),
        vmem((ROWS, wide, 128), BF16),
        vmem((keys, 6 * HD), BF16),
        vmem((keys, 4 * HD), BF16),
        vmem((128, keys), BF16),
        vmem((128, keys), BF16),
        vmem((ROWS, keys, wide), F32),
        vmem((ROWS, keys, wide), BF16),
        vmem((ROWS, keys, wide), BF16),
        vmem((ROWS, keys, wide), BF16),
        vmem((ROWS, keys, wide), BF16),
        vmem((2, wide, 128), F32),
        vmem((2, wide, 128), F32),
        vmem((group, 2, COLS, 128), F32),
        vmem((ny, nz, group, 128), F32),
        vmem((ny, nz, group, 128), F32),
        vmem((nz, group, 128), F32),
        vmem((nz, group, 128), F32),
        vmem((group, 1, 128), F32),
        vmem((group, 1, 128), F32),
        vmem((8, 128), F32),
        vmem((group, 8, 128), F32),
        vmem((8, 128), F32),
        vmem((ny, 8, 128), F32),
        vmem((8, 128), F32),
        vmem((nz, 8, 128), F32),
    ]
    counts = (
        group - 1, group - 1, group - 1, nz - 1, ny - 1, 8,
        group - 1, ny - 1, nz - 1, group - 1, group - 1, ny - 1, nz - 1,
    )
    for count in counts:
        scratch += [pltpu.SemaphoreType.DMA((count,)), pltpu.SemaphoreType.DMA((count,))]
    whole = pl.BlockSpec(memory_space=pltpu.VMEM)
    return pl.pallas_call(
        functools.partial(kernel, sizes),
        out_shape=(
            jax.ShapeDtypeStruct((ROWS, COLS, channels), F32),
            jax.ShapeDtypeStruct((1, channels), F32),
            jax.ShapeDtypeStruct((1, channels), F32),
            jax.ShapeDtypeStruct((9, channels), F32),
        ),
        in_specs=[pl.BlockSpec(memory_space=pltpu.HBM)] * 5,
        out_specs=(whole,) * 4,
        scratch_shapes=scratch,
        compiler_params=pltpu.CompilerParams(
            collective_id=0, has_side_effects=True, vmem_limit_bytes=48 << 20
        ),
    )(queries, cotangent, key_rows, value_rows, conv_taps)


def solution(mesh):
    sizes = (NX, NY, mesh.shape["lon"] // (2 * NX), mesh.shape["lat"] // NY)
    placed = (
        P("lat", "lon", None),
        P(("lat", "lon"), None),
        P(("lat", "lon"), None),
        P("lat", "lon", None),
        P(),
    )
    return jax.shard_map(
        functools.partial(body, sizes),
        mesh=mesh,
        in_specs=placed,
        out_specs=(P("lat", "lon", None), P(("lat", "lon"), None), P(("lat", "lon"), None), P()),
        check_vma=False,
    )
```

time: 69.5 us -> 67.2 us (0.967)
  Pallas kernels: 62.1 us -> 59.8 us
    pallas_call x1, Pallas kernels: 62.1 us -> 59.8 us  [body(): pl.pallas_call(functools.partial(kernel, sizes), out_shape=(jax.ShapeDtyp...]
where the time goes in v2:
time: 67.2 us; the launch traced here: 66.9 us
  Pallas kernels  59.8 us (89%)
  local copies, waits for them, and re-layouts  6.49 us (10%)
    pallas_call x1, Pallas kernels, body(): pl.pallas_call(functools.partial(kernel, sizes), out_shape=(jax.ShapeDtyp...  59.8 us
    unnamed x14, local copies, waits for them, and re-layouts  6.49 us

profile of v2, /device:TPU:1, one launch (start us, length us, event | category | flops | bytes accessed | tf_op | source)
XLA Modules:
  0.0 66.9 jit_solution(5095717751291965512)
XLA Ops:
  0.6 0.0 copy-start
  0.6 0.9 %copy-done = f32[4,32,512]{2,1,0:T(8,128)S(1)} copy-done((f32[4,32,512]{2,1,0:T(8,128)S(1)}, f32[4,32,512]{2,1,0:T(8,128)}, u32[]{:S(2)}) %copy-start) | copy-done | bytes 262168
  1.6 0.0 copy-start.1
  1.6 0.9 %copy-done.1 = f32[4,32,512]{2,1,0:T(8,128)S(1)} copy-done((f32[4,32,512]{2,1,0:T(8,128)S(1)}, f32[4,32,512]{2,1,0:T(8,128)}, u32[]{:S(2)}) %copy-start.1) | copy-done | bytes 262168
  2.5 0.0 copy-start.2
  2.5 0.8 %copy-done.2 = f32[9,512]{1,0:T(8,128)S(1)} copy-done((f32[9,512]{1,0:T(8,128)S(1)}, f32[9,512]{1,0:T(8,128)}, u32[]{:S(2)}) %copy-start.2) | copy-done | bytes 18456
  3.3 0.0 copy-start.3
  3.3 0.7 %copy-done.3 = f32[1,512]{1,0:T(1,128)S(1)} copy-done((f32[1,512]{1,0:T(1,128)S(1)}, f32[1,512]{1,0:T(1,128)}, u32[]{:S(2)}) %copy-start.3) | copy-done | bytes 2072
  4.0 0.0 copy-start.4
  4.0 0.7 %copy-done.4 = f32[1,512]{1,0:T(1,128)S(1)} copy-done((f32[1,512]{1,0:T(1,128)S(1)}, f32[1,512]{1,0:T(1,128)}, u32[]{:S(2)}) %copy-start.4) | copy-done | bytes 2072
  4.7 59.8 %shard_map.84 = (f32[4,32,512]{2,1,0:T(8,128)S(1)}, f32[1,512]{1,0:T(1,128)S(1)}, f32[1,512]{1,0:T(1,128)S(1)}, f32[9,512]{1,0:T(8,128)S(1)}) custom-call(f32[4,32,512]{2,1,0:T(8,128)S(1)} %copy-done, f32[4,32,512]{2,1,0:T(8,128)S(1)} %copy-done.1, f32[1,512]{1,0:T(1,128)S(1)} %copy-done.3, f32[1,512]{1,0:T(1,128)S(1)} %copy-done.4, f32[9,512]{1,0:T(8,128)S(1)} %copy-done.2), custom_call_target="tpu_custom_call" | custom-call | tf_op jit(solution)/shard_map/pallas_call | solution.py:488
  64.4 0.7 %copy.13 = f32[4,32,512]{2,1,0:T(8,128)} copy(f32[4,32,512]{2,1,0:T(8,128)S(1)} %get-tuple-element.8) | data formatting | bytes 524288
  65.1 0.6 copy.14
  65.7 0.6 copy.15
  66.3 0.6 copy.16
Async XLA Ops:
  0.6 1.0 %copy-start = (f32[4,32,512]{2,1,0:T(8,128)S(1)}, f32[4,32,512]{2,1,0:T(8,128)}, u32[]{:S(2)}) copy-start(f32[4,32,512]{2,1,0:T(8,128)} %q_hbm.1) | copy-start | bytes 786436
  1.6 0.9 %copy-start.1 = (f32[4,32,512]{2,1,0:T(8,128)S(1)}, f32[4,32,512]{2,1,0:T(8,128)}, u32[]{:S(2)}) copy-start(f32[4,32,512]{2,1,0:T(8,128)} %c_hbm.1) | copy-start | bytes 786436
  2.5 0.8 %copy-start.2 = (f32[9,512]{1,0:T(8,128)S(1)}, f32[9,512]{1,0:T(8,128)}, u32[]{:S(2)}) copy-start(f32[9,512]{1,0:T(8,128)} %t_hbm.1) | copy-start | bytes 55300
  3.3 0.7 %copy-start.3 = (f32[1,512]{1,0:T(1,128)S(1)}, f32[1,512]{1,0:T(1,128)}, u32[]{:S(2)}) copy-start(f32[1,512]{1,0:T(1,128)} %k_hbm.1) | copy-start | bytes 6148
  4.0 0.7 %copy-start.4 = (f32[1,512]{1,0:T(1,128)S(1)}, f32[1,512]{1,0:T(1,128)}, u32[]{:S(2)}) copy-start(f32[1,512]{1,0:T(1,128)} %v_hbm.1) | copy-start | bytes 6148

commit v3 on v2

v3 whole, which is shorter than its diff:
```python
import functools

import jax
import jax.numpy as jnp
import numpy as np
from jax import lax
from jax.experimental import pallas as pl
from jax.experimental.pallas import tpu as pltpu
from jax.sharding import PartitionSpec as P

HD = 64
NX = 4
NY = 4
ROWS = 4
COLS = 32
F32 = jnp.float32
BF16 = jnp.bfloat16
MESH = pl.DeviceIdType.MESH


def low_lanes(shape):
    return lax.broadcasted_iota(jnp.int32, shape, len(shape) - 1) < HD


def swap(value):
    return pltpu.roll(value, HD, value.ndim - 1)


def both_low(first, second):
    return jnp.where(low_lanes(first.shape), first, swap(second))


def both_high(first, second):
    return jnp.where(low_lanes(first.shape), swap(first), second)


def split2(value):
    high = value.astype(BF16)
    return high, (value - high.astype(F32)).astype(BF16)


def split3(value):
    first = value.astype(BF16)
    rest = value - first.astype(F32)
    second = rest.astype(BF16)
    return first, second, (rest - second.astype(F32)).astype(BF16)


def dot(a, b):
    return jnp.dot(a, b, preferred_element_type=F32)


def kernel(
    sizes,
    q_hbm, c_hbm, k_hbm, v_hbm, t_hbm,
    dq_ref, dk_ref, dv_ref, tu_ref,
    q_ref, c_ref, k_ref, v_ref, t_ref, in_s,
    ws, qs, wx, qx, kvz, ks, vs, kp, vp, hus, hds, hu, hd, hb,
    taps, bs, bd, rq, ro, ak, av, kt, vt, pf, ph, plo, dh, dlo, op, dqs, dqr,
    dvb, dkb, dvr, dkr, dvt, dkt, zs, rsz, tzs, tzr, txs, txr,
    w_s, w_r, q_s, q_r, z_s, z_r, k_s, k_r, v_s, v_r, u_s, u_r, n_s, n_r, h_s, h_r,
    d_s, d_r, rv_s, rv_r, rk_s, rk_r, rz_s, rz_r, tz_s, tz_r, tx_s, tx_r,
):
    nx, ny, nzl, nzh = sizes
    group = 2 * nx
    nz = nzl * nzh
    band_count = nzh * ny
    wide = group * COLS
    pairs = nz // 2
    keys_half = ny * group * pairs
    channels = group * HD
    lat = lax.axis_index("lat")
    lon = lax.axis_index("lon")
    y = lax.rem(lat, ny)
    z_hi = lax.div(lat, ny)
    z_lo = lax.div(lon, group)
    g = lax.rem(lon, group)
    z = z_hi * nzl + z_lo

    def at(z_of, y_of, g_of):
        return (lax.div(z_of, nzl) * ny + y_of, lax.rem(z_of, nzl) * group + g_of)

    def around(value, step, count):
        return lax.rem(value + step + count, count)

    x_peers = [at(z, y, around(g, e, group)) for e in range(1, group)]
    z_steps = sorted(range(1, nz), key=lambda e: -min(e, nz - e))
    z_peers = [at(around(z, e, nz), y, g) for e in z_steps]
    far = [(a, b) for a in range(ny) for b in range(group) if a or b]
    far = sorted(far, key=lambda s: -min(s[0], ny - s[0]) - min(s[1], group - s[1]) / 2)
    f_peers = [at(z, around(y, a, ny), around(g, b, group)) for a, b in far]

    def beside(d_lat, d_lon, to):
        return (around(lat, d_lat, band_count), around(z_lo, d_lon, nzl) * group + to)

    u_peers = [beside(1, 0, around(g, e, group)) for e in range(group)]
    n_peers = [beside(-1, 0, around(g, e, group)) for e in range(group)]
    h_steps = [(a, b) for a in (-1, 0, 1) for b in (1, -1)]
    h_peers = [beside(a, b, g) for a, b in h_steps]

    barrier = pltpu.get_barrier_semaphore()
    inputs = []
    for i, (source, target) in enumerate(
        ((k_hbm, k_ref), (v_hbm, v_ref), (c_hbm, c_ref), (q_hbm, q_ref), (t_hbm, t_ref))
    ):
        inputs.append(pltpu.make_async_copy(source, target, in_s.at[i]))
        inputs[i].start()
    partners = f_peers + z_peers + u_peers + n_peers + h_peers
    for peer in partners:
        pl.semaphore_signal(barrier, inc=1, device_id=peer, device_id_type=MESH)

    def send(source, target, send_sem, recv_sem, peer):
        copy = pltpu.make_async_remote_copy(
            src_ref=source, dst_ref=target, send_sem=send_sem, recv_sem=recv_sem,
            device_id=peer, device_id_type=MESH,
        )
        copy.start()
        started.append(copy)
        return copy

    started = []
    arrived = []

    def arrive(copies):
        for copy in copies:
            copy.wait_recv()
            arrived.append(copy)

    inputs[0].wait()
    inputs[1].wait()
    rows = []
    for m in range(group // 2):
        cut = slice(m * 128, (m + 1) * 128)
        rows.append(both_low(k_ref[:, cut], v_ref[:, cut]))
        rows.append(both_high(k_ref[:, cut], v_ref[:, cut]))
    own_z = pl.ds(pl.multiple_of(z * group, group), group)
    kvz[own_z] = jnp.concatenate(rows, 0)
    own_w = pl.multiple_of(8 + COLS * g, 8)
    own_q = pl.multiple_of(COLS * g, 8)

    pl.semaphore_wait(barrier, len(partners))

    z_copies = []
    for e, peer in enumerate(z_peers):
        z_copies.append(send(kvz.at[own_z], kvz.at[own_z], z_s.at[e], z_r.at[e], peer))

    inputs[2].wait()
    line_total = ROWS * band_count
    centres = (np.arange(line_total) + 0.5) * np.pi / line_total
    mean_cosine = float(np.mean(np.sin(centres)))
    line = lax.broadcasted_iota(jnp.int32, (8, 128), 0) + lat * ROWS
    weight = jnp.sin((line.astype(F32) + 0.5) * (np.pi / line_total)) / mean_cosine
    for m in range(group // 2):
        cut = slice(m * 128, (m + 1) * 128)
        for r in range(2):
            upper = c_ref[r, :, cut] * weight[r : r + 1]
            lower = c_ref[r + 2, :, cut] * weight[r + 2 : r + 3]
            ws[2 * m, r] = both_low(upper, lower)
            ws[2 * m + 1, r] = both_high(upper, lower)
            if r == 0:
                hds[2 * m] = both_low(upper[: COLS // 2], upper[COLS // 2 :])
                hds[2 * m + 1] = both_high(upper[: COLS // 2], upper[COLS // 2 :])
            else:
                hus[2 * m] = both_low(lower[: COLS // 2], lower[COLS // 2 :])
                hus[2 * m + 1] = both_high(lower[: COLS // 2], lower[COLS // 2 :])
    u_copies = []
    n_copies = []
    for e in range(group):
        to = around(g, e, group)
        u_copies.append(send(hus.at[to], hu.at[g], u_s.at[e], u_r.at[e], u_peers[e]))
        n_copies.append(send(hds.at[to], hd.at[g], n_s.at[e], n_r.at[e], n_peers[e]))
    w_copies = []
    for e, peer in enumerate(x_peers):
        to = around(g, e + 1, group)
        target = wx.at[pl.ds(1, 2), pl.ds(own_w, COLS), :]
        w_copies.append(send(ws.at[to], target, w_s.at[e], w_r.at[e], peer))
    wx[pl.ds(1, 2), pl.ds(own_w, COLS), :] = ws[g]
    inputs[3].wait()
    for m in range(group // 2):
        cut = slice(m * 128, (m + 1) * 128)
        for r in range(2):
            upper = q_ref[r, :, cut] * (HD ** -0.5)
            lower = q_ref[r + 2, :, cut] * (HD ** -0.5)
            qs[2 * m, r] = both_low(upper, lower)
            qs[2 * m + 1, r] = both_high(upper, lower)
    q_copies = []
    for e, peer in enumerate(x_peers):
        to = around(g, e + 1, group)
        target = qx.at[:, pl.ds(own_q, COLS), :]
        q_copies.append(send(qs.at[to], target, q_s.at[e], q_r.at[e], peer))
    qx[:, pl.ds(own_q, COLS), :] = qs[g]

    arrive(z_copies)
    for h in range(group):
        first = kvz[pl.ds(h, pairs, stride=group)]
        second = kvz[pl.ds(h + group * pairs, pairs, stride=group)]
        ks[h] = both_low(first, second)
        vs[h] = both_high(first, second)
    k_copies = []
    for e, peer in enumerate(f_peers):
        to = around(g, far[e][1], group)
        k_copies.append(send(ks.at[to], kp.at[y, g], k_s.at[e], k_r.at[e], peer))
    v_copies = []
    for e, peer in enumerate(f_peers):
        to = around(g, far[e][1], group)
        v_copies.append(send(vs.at[to], vp.at[y, g], v_s.at[e], v_r.at[e], peer))
    kp[y, g] = ks[g]
    vp[y, g] = vs[g]

    arrive(w_copies)
    h_copies = []
    for i, (a, b) in enumerate(h_steps):
        source = wx.at[pl.ds(1, 2), pl.ds(wide if b == 1 else 8, 8), :]
        h_copies.append(send(source, hb.at[i], h_s.at[i], h_r.at[i], h_peers[i]))

    arrive(q_copies)
    for r in range(2):
        value = qx[r]
        high = value.astype(BF16).astype(F32)
        low = value - high
        rq[r] = both_low(high, low).astype(BF16)
        rq[r + 2] = both_high(high, low).astype(BF16)
        q1, q2, q3 = split3(jnp.transpose(value))
        for part in range(2):
            rows = slice(part * HD, (part + 1) * HD)
            for place, piece in enumerate((q1, q2, q1, q2, q3, q1)):
                bs[r + 2 * part, place * HD : (place + 1) * HD] = piece[rows]

    pair = pl.multiple_of(lax.div(g, 2) * 128, 128)
    inputs[4].wait()
    taps[0:9] = t_ref[:, pl.ds(pair, 128)]
    taken = taps[...]
    low = low_lanes(taken.shape)
    even = jnp.where(low, taken, swap(taken))
    odd = jnp.where(low, swap(taken), taken)
    taps[...] = jnp.where(lax.rem(g, 2) == 0, even, odd)

    def wide_pieces(value):
        s1 = value.astype(BF16).astype(F32)
        rest = value - s1
        s2 = rest.astype(BF16).astype(F32)
        s3 = rest - s2
        low = low_lanes(value.shape)

        def both(a, b):
            first = jnp.where(low, a, swap(b)).astype(BF16)
            return first, jnp.where(low, swap(a), b).astype(BF16)

        return both(s1, s1), both(s2, s2), both(s1, s3)

    def turned_pieces(value, target):
        for i, piece in enumerate(split2(jnp.transpose(value))):
            target[i * HD : (i + 1) * HD, 0:keys_half] = piece[0:HD]
            target[i * HD : (i + 1) * HD, keys_half : 2 * keys_half] = piece[HD : 2 * HD]

    arrive(k_copies)
    value = kp[...].reshape(keys_half, 128)
    for i, (first, second) in enumerate(wide_pieces(value)):
        ak[0:keys_half, i * 128 : (i + 1) * 128] = first
        ak[keys_half : 2 * keys_half, i * 128 : (i + 1) * 128] = second
    turned_pieces(value, kt)

    out_parts = []
    for r in range(ROWS):
        logits = dot(ak[...], bs[r])
        raised = jnp.exp(logits - jnp.max(logits, 0, keepdims=True))
        soft = raised * (1.0 / jnp.sum(raised, 0, keepdims=True))
        soft_high, soft_low = split2(soft)
        pf[r] = soft
        ph[r] = soft_high
        plo[r] = soft_low

    arrive(v_copies)
    value = vp[...].reshape(keys_half, 128)
    for i, (first, second) in enumerate(wide_pieces(value)[0:2]):
        av[0:keys_half, i * 128 : (i + 1) * 128] = first
        av[keys_half : 2 * keys_half, i * 128 : (i + 1) * 128] = second
    turned_pieces(value, vt)
    for r in range(ROWS):
        both = dot(vt[...], ph[r]) + dot(vt[...], plo[r])
        out_parts.append(both[0:HD] + both[HD : 2 * HD])
    for r in range(2):
        op[r] = jnp.transpose(jnp.concatenate([out_parts[r], out_parts[r + 2]], 0))

    arrive(h_copies + u_copies + n_copies)
    slot = {step: i for i, step in enumerate(h_steps)}
    left, right = 7, 8 + wide
    for r in range(2):
        wx[r + 1, left : left + 1] = hb[slot[0, 1], r, 7:8]
        wx[r + 1, right : right + 1] = hb[slot[0, -1], r, 0:1]
    top = jnp.where(lat > 0, 1.0, 0.0)
    bottom = jnp.where(lat < band_count - 1, 1.0, 0.0)

    def above(low_part, own):
        return jnp.where(low_lanes(own.shape), low_part * top, swap(own))

    def below(own, high_part):
        return jnp.where(low_lanes(own.shape), swap(own), high_part * bottom)

    part = COLS // 2
    for j in range(group):
        one = slice(8 + COLS * j, 8 + COLS * j + part)
        two = slice(8 + COLS * j + part, 8 + COLS * (j + 1))
        wx[0, one] = above(hu[j], wx[2, one])
        wx[0, two] = above(swap(hu[j]), wx[2, two])
        wx[3, one] = below(wx[1, one], swap(hd[j]))
        wx[3, two] = below(wx[1, two], hd[j])
    wx[0, left : left + 1] = above(swap(hb[slot[1, 1], 1, 7:8]), wx[2, left : left + 1])
    wx[0, right : right + 1] = above(swap(hb[slot[1, -1], 1, 0:1]), wx[2, right : right + 1])
    wx[3, left : left + 1] = below(wx[1, left : left + 1], swap(hb[slot[-1, 1], 0, 7:8]))
    wx[3, right : right + 1] = below(wx[1, right : right + 1], swap(hb[slot[-1, -1], 0, 0:1]))

    for r in range(2):
        value = wx[r + 1, 8 : 8 + wide]
        for a in (-1, 0, 1):
            for b in (-1, 0, 1):
                tap = 3 * (a + 1) + (b + 1)
                value = value + taps[tap : tap + 1] * wx[r + 1 - a, 8 - b : 8 - b + wide]
        high = value.astype(BF16).astype(F32)
        low = value - high
        ro[r] = both_low(high, low).astype(BF16)
        ro[r + 2] = both_high(high, low).astype(BF16)
        o1, o2 = split2(jnp.transpose(value))
        for part in range(2):
            rows = slice(part * HD, (part + 1) * HD)
            for place, piece in enumerate((o1, o2, o1, o2)):
                bd[r + 2 * part, place * HD : (place + 1) * HD] = piece[rows]

    sums = []
    for a in (-1, 0, 1):
        for b in (-1, 0, 1):
            total = jnp.sum(
                op[0] * wx[1 - a, 8 - b : 8 - b + wide]
                + op[1] * wx[2 - a, 8 - b : 8 - b + wide],
                0,
                keepdims=True,
            )
            sums.append(total + swap(total))
    first = jnp.concatenate(sums[0:8], 0)
    line = lax.broadcasted_iota(jnp.int32, (8, 128), 0)
    last = jnp.where(line == 0, jnp.broadcast_to(sums[8], (8, 128)), 0.0)
    tap_tile = jnp.where(low_lanes((8, 128)), first, last)

    tzs[...] = tap_tile
    tz_copies = []
    for e, peer in enumerate(z_peers):
        tz_copies.append(send(tzs, tzr.at[z], tz_s.at[e], tz_r.at[e], peer))
    tzr[z] = tap_tile

    def summed(highs, lows, right):
        total = dot(highs[0], right[0]) + dot(lows[0], right[0])
        for r in range(1, ROWS):
            total = total + dot(highs[r], right[r]) + dot(lows[r], right[r])
        total = total + swap(total)
        first = total[0:keys_half]
        total = jnp.where(low_lanes(first.shape), first, total[keys_half : 2 * keys_half])
        return total.reshape(ny, group, pairs, 128)

    def spread(source, target, send_sems, recv_sems):
        copies = []
        for e, peer in enumerate(f_peers):
            a, b = far[e]
            block = source.at[around(y, a, ny), around(g, b, group)]
            copies.append(send(block, target.at[y, g], send_sems.at[e], recv_sems.at[e], peer))
        target[y, g] = source[y, g]
        return copies

    dvb[...] = summed(ph, plo, ro)
    rv_copies = spread(dvb, dvr, rv_s, rv_r)

    query_parts = []
    for r in range(ROWS):
        soft = pf[r]
        prob_grad = dot(av[...], bd[r])
        row_dot = jnp.sum(soft * prob_grad, 0, keepdims=True)
        grad_high, grad_low = split2(soft * (prob_grad - row_dot))
        dh[r] = grad_high
        dlo[r] = grad_low
        both = dot(kt[...], grad_high) + dot(kt[...], grad_low)
        query_parts.append((both[0:HD] + both[HD : 2 * HD]) * (HD ** -0.5))

    dkb[...] = summed(dh, dlo, rq)
    rk_copies = spread(dkb, dkr, rk_s, rk_r)

    for r in range(2):
        dqs[r] = jnp.transpose(jnp.concatenate([query_parts[r], query_parts[r + 2]], 0))
    d_copies = []
    for e, peer in enumerate(x_peers):
        to = pl.multiple_of(around(g, e + 1, group) * COLS, 8)
        source = dqs.at[:, pl.ds(to, COLS), :]
        d_copies.append(send(source, dqr.at[g], d_s.at[e], d_r.at[e], peer))
    dqr[g] = dqs[:, pl.ds(own_q, COLS), :]

    arrive(tz_copies)
    total = tzr[0]
    for i in range(1, nz):
        total = total + tzr[i]
    txs[...] = total
    tx_copies = []
    for e, peer in enumerate(f_peers):
        tx_copies.append(send(txs, txr.at[y, g], tx_s.at[e], tx_r.at[e], peer))
    txr[y, g] = total

    arrive(rv_copies)
    total = dvr[0]
    for i in range(1, ny):
        total = total + dvr[i]
    dvt[...] = total.reshape(group * pairs, 128)
    arrive(rk_copies)
    total = dkr[0]
    for i in range(1, ny):
        total = total + dkr[i]
    dkt[...] = total.reshape(group * pairs, 128)
    for i in range(pairs):
        key_part = dkt[pl.ds(i, group, stride=pairs)]
        value_part = dvt[pl.ds(i, group, stride=pairs)]
        zs[i] = both_low(key_part, value_part)
        zs[i + pairs] = both_high(key_part, value_part)
    rz_copies = []
    for e, peer in enumerate(z_peers):
        to = around(z, z_steps[e], nz)
        rz_copies.append(send(zs.at[to], rsz.at[z], rz_s.at[e], rz_r.at[e], peer))
    rsz[z] = zs[z]

    arrive(d_copies)
    for m in range(group // 2):
        cut = slice(m * 128, (m + 1) * 128)
        for r in range(2):
            dq_ref[r, :, cut] = both_low(dqr[2 * m, r], dqr[2 * m + 1, r])
            dq_ref[r + 2, :, cut] = both_high(dqr[2 * m, r], dqr[2 * m + 1, r])

    arrive(tx_copies)
    tiles = []
    for j in range(group):
        total = txr[0, j]
        for i in range(1, ny):
            total = total + txr[i, j]
        tiles.append(total)
    square = tiles[0] * tiles[0]
    for tile in tiles[1:]:
        square = square + tile * tile
    mean = jnp.sum(square) * (1.0 / (9 * channels))
    scale = jnp.sqrt(jnp.full((8, 128), mean, F32) + 1e-6)
    for m in range(group // 2):
        cut = slice(m * 128, (m + 1) * 128)
        one, two = tiles[2 * m], tiles[2 * m + 1]
        tu_ref[0:8, cut] = both_low(one, two) / scale
        tu_ref[8:9, cut] = (both_high(one, two) / scale)[0:1]

    arrive(rz_copies)
    total = rsz[0]
    for i in range(1, nz):
        total = total + rsz[i]
    for m in range(group // 2):
        cut = slice(m * 128, (m + 1) * 128)
        one, two = total[2 * m : 2 * m + 1], total[2 * m + 1 : 2 * m + 2]
        dk_ref[:, cut] = both_low(one, two)
        dv_ref[:, cut] = both_high(one, two)
    for copy in started:
        copy.wait_send()


def leave(*refs):
    count = len(refs) // 2
    sems = refs[-1]
    copies = []
    for i in range(count):
        copies.append(pltpu.make_async_copy(refs[i], refs[count + i], sems.at[i]))
        copies[i].start()
    for copy in copies:
        copy.wait()


def put_out(results):
    count = len(results)
    return pl.pallas_call(
        leave,
        out_shape=tuple(jax.ShapeDtypeStruct(r.shape, r.dtype) for r in results),
        in_specs=[pl.BlockSpec(memory_space=pltpu.VMEM)] * count,
        out_specs=(pl.BlockSpec(memory_space=pltpu.HBM),) * count,
        scratch_shapes=[pltpu.SemaphoreType.DMA((count,))],
    )(*[pltpu.with_memory_space_constraint(r, pltpu.VMEM) for r in results])


def body(sizes, queries, key_rows, value_rows, cotangent, conv_taps):
    nx, ny, nzl, nzh = sizes
    group = 2 * nx
    nz = nzl * nzh
    wide = group * COLS
    keys = ny * nz * group
    pairs = nz // 2
    channels = group * HD
    vmem = pltpu.VMEM
    scratch = [
        vmem((ROWS, COLS, channels), F32),
        vmem((ROWS, COLS, channels), F32),
        vmem((1, channels), F32),
        vmem((1, channels), F32),
        vmem((9, channels), F32),
        pltpu.SemaphoreType.DMA((5,)),
        vmem((group, 2, COLS, 128), F32),
        vmem((group, 2, COLS, 128), F32),
        vmem((4, wide + 16, 128), F32),
        vmem((2, wide, 128), F32),
        vmem((nz * group, 128), F32),
        vmem((group, pairs, 128), F32),
        vmem((group, pairs, 128), F32),
        vmem((ny, group, pairs, 128), F32),
        vmem((ny, group, pairs, 128), F32),
        vmem((group, COLS // 2, 128), F32),
        vmem((group, COLS // 2, 128), F32),
        vmem((group, COLS // 2, 128), F32),
        vmem((group, COLS // 2, 128), F32),
        vmem((6, 2, 8, 128), F32),
        vmem((16, 128), F32),
        vmem((ROWS, 6 * HD, wide), BF16),
        vmem((ROWS, 4 * HD, wide), BF16),
        vmem((ROWS, wide, 128), BF16),
        vmem((ROWS, wide, 128), BF16),
        vmem((keys, 6 * HD), BF16),
        vmem((keys, 4 * HD), BF16),
        vmem((128, keys), BF16),
        vmem((128, keys), BF16),
        vmem((ROWS, keys, wide), F32),
        vmem((ROWS, keys, wide), BF16),
        vmem((ROWS, keys, wide), BF16),
        vmem((ROWS, keys, wide), BF16),
        vmem((ROWS, keys, wide), BF16),
        vmem((2, wide, 128), F32),
        vmem((2, wide, 128), F32),
        vmem((group, 2, COLS, 128), F32),
        vmem((ny, group, pairs, 128), F32),
        vmem((ny, group, pairs, 128), F32),
        vmem((ny, group, pairs, 128), F32),
        vmem((ny, group, pairs, 128), F32),
        vmem((group * pairs, 128), F32),
        vmem((group * pairs, 128), F32),
        vmem((nz, group, 128), F32),
        vmem((nz, group, 128), F32),
        vmem((8, 128), F32),
        vmem((nz, 8, 128), F32),
        vmem((8, 128), F32),
        vmem((ny, group, 8, 128), F32),
    ]
    plane = ny * group - 1
    counts = (
        group - 1, group - 1, nz - 1, plane, plane, group, group, 6,
        group - 1, plane, plane, nz - 1, nz - 1, plane,
    )
    for count in counts:
        scratch += [pltpu.SemaphoreType.DMA((count,)), pltpu.SemaphoreType.DMA((count,))]
    whole = pl.BlockSpec(memory_space=pltpu.VMEM)
    results = pl.pallas_call(
        functools.partial(kernel, sizes),
        out_shape=(
            jax.ShapeDtypeStruct((ROWS, COLS, channels), F32),
            jax.ShapeDtypeStruct((1, channels), F32),
            jax.ShapeDtypeStruct((1, channels), F32),
            jax.ShapeDtypeStruct((9, channels), F32),
        ),
        in_specs=[pl.BlockSpec(memory_space=pltpu.HBM)] * 5,
        out_specs=(whole,) * 4,
        scratch_shapes=scratch,
        compiler_params=pltpu.CompilerParams(
            collective_id=0, has_side_effects=True, vmem_limit_bytes=48 << 20
        ),
    )(*[pltpu.with_memory_space_constraint(a, pltpu.HBM) for a in (queries, cotangent, key_rows, value_rows, conv_taps)])
    return put_out(results)


def solution(mesh):
    sizes = (NX, NY, mesh.shape["lon"] // (2 * NX), mesh.shape["lat"] // NY)
    placed = (
        P("lat", "lon", None),
        P(("lat", "lon"), None),
        P(("lat", "lon"), None),
        P("lat", "lon", None),
        P(),
    )
    return jax.shard_map(
        functools.partial(body, sizes),
        mesh=mesh,
        in_specs=placed,
        out_specs=(P("lat", "lon", None), P(("lat", "lon"), None), P(("lat", "lon"), None), P()),
        check_vma=False,
    )
```

time: 67.2 us -> 56.8 us (0.85)
  local copies, waits for them, and re-layouts: 6.49 us -> 0 us
  Pallas kernels: 59.8 us -> 56 us
    unnamed x14 -> x0, local copies, waits for them, and re-layouts: 6.49 us -> none
    pallas_call x1, Pallas kernels: 59.8 us -> 55.2 us  [body(): pl.pallas_call(functools.partial(kernel, sizes), out_shape=(jax.ShapeDtyp...]
    pallas_call x0 -> x1, Pallas kernels: none -> 0.75 us  [put_out(): pl.pallas_call(leave, out_shape=tuple((jax.ShapeDtypeStruct(r.shape, r.dt...]
where the time goes in v3:
time: 56.8 us; the launch traced here: 56.6 us
  Pallas kernels  56 us (99%)
  between operations  0.64 us (1%)
    pallas_call x1, Pallas kernels, body(): pl.pallas_call(functools.partial(kernel, sizes), out_shape=(jax.ShapeDtyp...  55.2 us

profile of v3, /device:TPU:1, one launch (start us, length us, event | category | flops | bytes accessed | tf_op | source)
XLA Modules:
  0.0 56.6 jit_solution(11450031577009639150)
XLA Ops:
  0.6 55.2 %shard_map.84 = (f32[4,32,512]{2,1,0:T(8,128)S(1)}, f32[1,512]{1,0:T(1,128)S(1)}, f32[1,512]{1,0:T(1,128)S(1)}, f32[9,512]{1,0:T(8,128)S(1)}) custom-call(f32[4,32,512]{2,1,0:T(8,128)} %q_hbm.1, f32[4,32,512]{2,1,0:T(8,128)} %c_hbm.1, f32[1,512]{1,0:T(1,128)} %k_hbm.1, f32[1,512]{1,0:T(1,128)} %v_hbm.1, f32[9,512]{1,0:T(8,128)} %t_hbm.1), custom_call_target="tpu_custom_call" | custom-call | tf_op jit(solution)/shard_map/pallas_call | solution.py:553
  55.9 0.7 %shard_map.85 = (f32[4,32,512]{2,1,0:T(8,128)}, f32[1,512]{1,0:T(1,128)}, f32[1,512]{1,0:T(1,128)}, f32[9,512]{1,0:T(8,128)}) custom-call(f32[4,32,512]{2,1,0:T(8,128)S(1)} %get-tuple-element.8.refs_0_, f32[1,512]{1,0:T(1,128)S(1)} %get-tuple-element.9.refs_1_, f32[1,512]{1,0:T(1,128)S(1)} %get-tuple-element.10.refs_2_, f32[9,512]{1,0:T(8,128)S(1)} %get-tuple-element.11.refs_3_), custom_call_target="tpu_custom_call" | custom-call | tf_op jit(solution)/shard_map/pallas_call | solution.py:476

commit v4 on v3

--- a/solution.py
+++ b/solution.py
@@ -59,7 +59,7 @@
     taps, bs, bd, rq, ro, ak, av, kt, vt, pf, ph, plo, dh, dlo, op, dqs, dqr,
     dvb, dkb, dvr, dkr, dvt, dkt, zs, rsz, tzs, tzr, txs, txr,
     w_s, w_r, q_s, q_r, z_s, z_r, k_s, k_r, v_s, v_r, u_s, u_r, n_s, n_r, h_s, h_r,
-    d_s, d_r, rv_s, rv_r, rk_s, rk_r, rz_s, rz_r, tz_s, tz_r, tx_s, tx_r,
+    d_s, d_r, rv_s, rv_r, rk_s, rk_r, rz_s, rz_r, tz_s, tz_r, tx_s, tx_r, met,
 ):
     nx, ny, nzl, nzh = sizes
     group = 2 * nx
@@ -76,6 +76,8 @@
     z_lo = lax.div(lon, group)
     g = lax.rem(lon, group)
     z = z_hi * nzl + z_lo
+    here = y * group + g
+    plane = ny * group - 1
 
     def at(z_of, y_of, g_of):
         return (lax.div(z_of, nzl) * ny + y_of, lax.rem(z_of, nzl) * group + g_of)
@@ -105,7 +107,10 @@
     ):
         inputs.append(pltpu.make_async_copy(source, target, in_s.at[i]))
         inputs[i].start()
-    partners = f_peers + z_peers + u_peers + n_peers + h_peers
+    y_peers = [at(z, around(y, e, ny), g) for e in range(1, ny)]
+    bands = [beside(1, 0, g), beside(-1, 0, g)]
+    sides = [beside(0, 1, g), beside(0, -1, g)]
+    partners = z_peers + bands + y_peers + x_peers
     for peer in partners:
         pl.semaphore_signal(barrier, inc=1, device_id=peer, device_id_type=MESH)
 
@@ -115,16 +120,22 @@
             device_id=peer, device_id_type=MESH,
         )
         copy.start()
-        started.append(copy)
-        return copy
 
     started = []
     arrived = []
 
-    def arrive(copies):
-        for copy in copies:
-            copy.wait_recv()
-            arrived.append(copy)
+    def phase(block, send_sem, recv_sem):
+        copies = pltpu.make_async_remote_copy(
+            src_ref=block, dst_ref=block, send_sem=send_sem, recv_sem=recv_sem,
+            device_id=x_peers[0], device_id_type=MESH,
+        )
+        started.append(copies)
+        return copies
+
+    def arrive(*phases):
+        for copies in phases:
+            copies.wait_recv()
+            arrived.append(copies)
 
     inputs[0].wait()
     inputs[1].wait()
@@ -140,9 +151,12 @@
 
     pl.semaphore_wait(barrier, len(partners))
 
-    z_copies = []
+    z_copies = phase(kvz.at[pl.ds(0, (nz - 1) * group)], z_s, z_r)
     for e, peer in enumerate(z_peers):
-        z_copies.append(send(kvz.at[own_z], kvz.at[own_z], z_s.at[e], z_r.at[e], peer))
+        send(kvz.at[own_z], kvz.at[own_z], z_s, z_r, peer)
+    relays = bands + y_peers + sides
+    for peer in relays:
+        pl.semaphore_signal(met, inc=1, device_id=peer, device_id_type=MESH)
 
     inputs[2].wait()
     line_total = ROWS * band_count
@@ -163,17 +177,11 @@
             else:
                 hus[2 * m] = both_low(lower[: COLS // 2], lower[COLS // 2 :])
                 hus[2 * m + 1] = both_high(lower[: COLS // 2], lower[COLS // 2 :])
-    u_copies = []
-    n_copies = []
-    for e in range(group):
-        to = around(g, e, group)
-        u_copies.append(send(hus.at[to], hu.at[g], u_s.at[e], u_r.at[e], u_peers[e]))
-        n_copies.append(send(hds.at[to], hd.at[g], n_s.at[e], n_r.at[e], n_peers[e]))
-    w_copies = []
+    w_copies = phase(ws.at[pl.ds(0, group - 1)], w_s, w_r)
     for e, peer in enumerate(x_peers):
         to = around(g, e + 1, group)
         target = wx.at[pl.ds(1, 2), pl.ds(own_w, COLS), :]
-        w_copies.append(send(ws.at[to], target, w_s.at[e], w_r.at[e], peer))
+        send(ws.at[to], target, w_s, w_r, peer)
     wx[pl.ds(1, 2), pl.ds(own_w, COLS), :] = ws[g]
     inputs[3].wait()
     for m in range(group // 2):
@@ -183,12 +191,19 @@
             lower = q_ref[r + 2, :, cut] * (HD ** -0.5)
             qs[2 * m, r] = both_low(upper, lower)
             qs[2 * m + 1, r] = both_high(upper, lower)
-    q_copies = []
+    q_copies = phase(qs.at[pl.ds(0, group - 1)], q_s, q_r)
     for e, peer in enumerate(x_peers):
         to = around(g, e + 1, group)
         target = qx.at[:, pl.ds(own_q, COLS), :]
-        q_copies.append(send(qs.at[to], target, q_s.at[e], q_r.at[e], peer))
+        send(qs.at[to], target, q_s, q_r, peer)
     qx[:, pl.ds(own_q, COLS), :] = qs[g]
+    pl.semaphore_wait(met, len(relays))
+    u_copies = phase(hu, u_s, u_r)
+    n_copies = phase(hd, n_s, n_r)
+    for e in range(group):
+        to = around(g, e, group)
+        send(hus.at[to], hu.at[g], u_s, u_r, u_peers[e])
+        send(hds.at[to], hd.at[g], n_s, n_r, n_peers[e])
 
     arrive(z_copies)
     for h in range(group):
@@ -196,22 +211,22 @@
         second = kvz[pl.ds(h + group * pairs, pairs, stride=group)]
         ks[h] = both_low(first, second)
         vs[h] = both_high(first, second)
-    k_copies = []
+    k_copies = phase(kp.at[pl.ds(0, plane)], k_s, k_r)
     for e, peer in enumerate(f_peers):
         to = around(g, far[e][1], group)
-        k_copies.append(send(ks.at[to], kp.at[y, g], k_s.at[e], k_r.at[e], peer))
-    v_copies = []
+        send(ks.at[to], kp.at[here], k_s, k_r, peer)
+    v_copies = phase(vp.at[pl.ds(0, plane)], v_s, v_r)
     for e, peer in enumerate(f_peers):
         to = around(g, far[e][1], group)
-        v_copies.append(send(vs.at[to], vp.at[y, g], v_s.at[e], v_r.at[e], peer))
-    kp[y, g] = ks[g]
-    vp[y, g] = vs[g]
+        send(vs.at[to], vp.at[here], v_s, v_r, peer)
+    kp[here] = ks[g]
+    vp[here] = vs[g]
 
     arrive(w_copies)
-    h_copies = []
+    h_copies = phase(hb, h_s, h_r)
     for i, (a, b) in enumerate(h_steps):
         source = wx.at[pl.ds(1, 2), pl.ds(wide if b == 1 else 8, 8), :]
-        h_copies.append(send(source, hb.at[i], h_s.at[i], h_r.at[i], h_peers[i]))
+        send(source, hb.at[i], h_s, h_r, h_peers[i])
 
     arrive(q_copies)
     for r in range(2):
@@ -282,7 +297,7 @@
     for r in range(2):
         op[r] = jnp.transpose(jnp.concatenate([out_parts[r], out_parts[r + 2]], 0))
 
-    arrive(h_copies + u_copies + n_copies)
+    arrive(h_copies, u_copies, n_copies)
     slot = {step: i for i, step in enumerate(h_steps)}
     left, right = 7, 8 + wide
     for r in range(2):
@@ -342,9 +357,9 @@
     tap_tile = jnp.where(low_lanes((8, 128)), first, last)
 
     tzs[...] = tap_tile
-    tz_copies = []
+    tz_copies = phase(tzr.at[pl.ds(0, nz - 1)], tz_s, tz_r)
     for e, peer in enumerate(z_peers):
-        tz_copies.append(send(tzs, tzr.at[z], tz_s.at[e], tz_r.at[e], peer))
+        send(tzs, tzr.at[z], tz_s, tz_r, peer)
     tzr[z] = tap_tile
 
     def summed(highs, lows, right):
@@ -354,15 +369,15 @@
         total = total + swap(total)
         first = total[0:keys_half]
         total = jnp.where(low_lanes(first.shape), first, total[keys_half : 2 * keys_half])
-        return total.reshape(ny, group, pairs, 128)
-
-    def spread(source, target, send_sems, recv_sems):
-        copies = []
+        return total.reshape(ny * group, pairs, 128)
+
+    def spread(source, target, send_sem, recv_sem):
+        copies = phase(target.at[pl.ds(0, plane)], send_sem, recv_sem)
         for e, peer in enumerate(f_peers):
             a, b = far[e]
-            block = source.at[around(y, a, ny), around(g, b, group)]
-            copies.append(send(block, target.at[y, g], send_sems.at[e], recv_sems.at[e], peer))
-        target[y, g] = source[y, g]
+            block = source.at[around(y, a, ny) * group + around(g, b, group)]
+            send(block, target.at[here], send_sem, recv_sem, peer)
+        target[here] = source[here]
         return copies
 
     dvb[...] = summed(ph, plo, ro)
@@ -384,11 +399,11 @@
 
     for r in range(2):
         dqs[r] = jnp.transpose(jnp.concatenate([query_parts[r], query_parts[r + 2]], 0))
-    d_copies = []
+    d_copies = phase(dqr.at[pl.ds(0, group - 1)], d_s, d_r)
     for e, peer in enumerate(x_peers):
         to = pl.multiple_of(around(g, e + 1, group) * COLS, 8)
         source = dqs.at[:, pl.ds(to, COLS), :]
-        d_copies.append(send(source, dqr.at[g], d_s.at[e], d_r.at[e], peer))
+        send(source, dqr.at[g], d_s, d_r, peer)
     dqr[g] = dqs[:, pl.ds(own_q, COLS), :]
 
     arrive(tz_copies)
@@ -396,30 +411,30 @@
     for i in range(1, nz):
         total = total + tzr[i]
     txs[...] = total
-    tx_copies = []
+    tx_copies = phase(txr.at[pl.ds(0, plane)], tx_s, tx_r)
     for e, peer in enumerate(f_peers):
-        tx_copies.append(send(txs, txr.at[y, g], tx_s.at[e], tx_r.at[e], peer))
-    txr[y, g] = total
+        send(txs, txr.at[here], tx_s, tx_r, peer)
+    txr[here] = total
 
     arrive(rv_copies)
-    total = dvr[0]
+    total = dvr[0:group]
     for i in range(1, ny):
-        total = total + dvr[i]
+        total = total + dvr[i * group : (i + 1) * group]
     dvt[...] = total.reshape(group * pairs, 128)
     arrive(rk_copies)
-    total = dkr[0]
+    total = dkr[0:group]
     for i in range(1, ny):
-        total = total + dkr[i]
+        total = total + dkr[i * group : (i + 1) * group]
     dkt[...] = total.reshape(group * pairs, 128)
     for i in range(pairs):
         key_part = dkt[pl.ds(i, group, stride=pairs)]
         value_part = dvt[pl.ds(i, group, stride=pairs)]
         zs[i] = both_low(key_part, value_part)
         zs[i + pairs] = both_high(key_part, value_part)
-    rz_copies = []
+    rz_copies = phase(rsz.at[pl.ds(0, nz - 1)], rz_s, rz_r)
     for e, peer in enumerate(z_peers):
         to = around(z, z_steps[e], nz)
-        rz_copies.append(send(zs.at[to], rsz.at[z], rz_s.at[e], rz_r.at[e], peer))
+        send(zs.at[to], rsz.at[z], rz_s, rz_r, peer)
     rsz[z] = zs[z]
 
     arrive(d_copies)
@@ -432,9 +447,9 @@
     arrive(tx_copies)
     tiles = []
     for j in range(group):
-        total = txr[0, j]
+        total = txr[j]
         for i in range(1, ny):
-            total = total + txr[i, j]
+            total = total + txr[i * group + j]
         tiles.append(total)
     square = tiles[0] * tiles[0]
     for tile in tiles[1:]:
@@ -505,8 +520,8 @@
         vmem((nz * group, 128), F32),
         vmem((group, pairs, 128), F32),
         vmem((group, pairs, 128), F32),
-        vmem((ny, group, pairs, 128), F32),
-        vmem((ny, group, pairs, 128), F32),
+        vmem((ny * group, pairs, 128), F32),
+        vmem((ny * group, pairs, 128), F32),
         vmem((group, COLS // 2, 128), F32),
         vmem((group, COLS // 2, 128), F32),
         vmem((group, COLS // 2, 128), F32),
@@ -529,10 +544,10 @@
         vmem((2, wide, 128), F32),
         vmem((2, wide, 128), F32),
         vmem((group, 2, COLS, 128), F32),
-        vmem((ny, group, pairs, 128), F32),
-        vmem((ny, group, pairs, 128), F32),
-        vmem((ny, group, pairs, 128), F32),
-        vmem((ny, group, pairs, 128), F32),
+        vmem((ny * group, pairs, 128), F32),
+        vmem((ny * group, pairs, 128), F32),
+        vmem((ny * group, pairs, 128), F32),
+        vmem((ny * group, pairs, 128), F32),
         vmem((group * pairs, 128), F32),
         vmem((group * pairs, 128), F32),
         vmem((nz, group, 128), F32),
@@ -540,15 +555,10 @@
         vmem((8, 128), F32),
         vmem((nz, 8, 128), F32),
         vmem((8, 128), F32),
-        vmem((ny, group, 8, 128), F32),
+        vmem((ny * group, 8, 128), F32),
     ]
-    plane = ny * group - 1
-    counts = (
-        group - 1, group - 1, nz - 1, plane, plane, group, group, 6,
-        group - 1, plane, plane, nz - 1, nz - 1, plane,
-    )
-    for count in counts:
-        scratch += [pltpu.SemaphoreType.DMA((count,)), pltpu.SemaphoreType.DMA((count,))]
+    scratch += [pltpu.SemaphoreType.DMA] * 28
+    scratch.append(pltpu.SemaphoreType.REGULAR)
     whole = pl.BlockSpec(memory_space=pltpu.VMEM)
     results = pl.pallas_call(
         functools.partial(kernel, sizes),

time: 56.8 us -> 51 us (0.90)
  Pallas kernels: 56 us -> 50.2 us
    pallas_call x1, Pallas kernels: 55.2 us -> 49.5 us  [body(): pl.pallas_call(functools.partial(kernel, sizes), out_shape=(jax.ShapeDtyp...]
where the time goes in v4:
time: 51 us; the launch traced here: 50.9 us
  Pallas kernels  50.2 us (98%)
  between operations  0.64 us (1%)
    pallas_call x1, Pallas kernels, body(): pl.pallas_call(functools.partial(kernel, sizes), out_shape=(jax.ShapeDtyp...  49.5 us

profile of v4, /device:TPU:1, one launch (start us, length us, event | category | flops | bytes accessed | tf_op | source)
XLA Modules:
  0.0 50.9 jit_solution(2204632308590358621)
XLA Ops:
  0.6 49.5 %shard_map.84 = (f32[4,32,512]{2,1,0:T(8,128)S(1)}, f32[1,512]{1,0:T(1,128)S(1)}, f32[1,512]{1,0:T(1,128)S(1)}, f32[9,512]{1,0:T(8,128)S(1)}) custom-call(f32[4,32,512]{2,1,0:T(8,128)} %q_hbm.1, f32[4,32,512]{2,1,0:T(8,128)} %c_hbm.1, f32[1,512]{1,0:T(1,128)} %k_hbm.1, f32[1,512]{1,0:T(1,128)} %v_hbm.1, f32[9,512]{1,0:T(8,128)} %t_hbm.1), custom_call_target="tpu_custom_call" | custom-call | tf_op jit(solution)/shard_map/pallas_call | solution.py:563
  50.1 0.7 %shard_map.85 = (f32[4,32,512]{2,1,0:T(8,128)}, f32[1,512]{1,0:T(1,128)}, f32[1,512]{1,0:T(1,128)}, f32[9,512]{1,0:T(8,128)}) custom-call(f32[4,32,512]{2,1,0:T(8,128)S(1)} %get-tuple-element.8.refs_0_, f32[1,512]{1,0:T(1,128)S(1)} %get-tuple-element.9.refs_1_, f32[1,512]{1,0:T(1,128)S(1)} %get-tuple-element.10.refs_2_, f32[9,512]{1,0:T(8,128)S(1)} %get-tuple-element.11.refs_3_), custom_call_target="tpu_custom_call" | custom-call | tf_op jit(solution)/shard_map/pallas_call | solution.py:491

commit v5 on v4

--- a/solution.py
+++ b/solution.py
@@ -89,7 +89,7 @@
     z_steps = sorted(range(1, nz), key=lambda e: -min(e, nz - e))
     z_peers = [at(around(z, e, nz), y, g) for e in z_steps]
     far = [(a, b) for a in range(ny) for b in range(group) if a or b]
-    far = sorted(far, key=lambda s: -min(s[0], ny - s[0]) - min(s[1], group - s[1]) / 2)
+    far = sorted(far, key=lambda s: min(s[0], ny - s[0]) + min(s[1], group - s[1]) / 2)
     f_peers = [at(z, around(y, a, ny), around(g, b, group)) for a, b in far]
 
     def beside(d_lat, d_lon, to):

time: 51 us -> 50.6 us (level)
  no operation moved by 1% of the time
where the time goes in v5:
time: 50.6 us; the launch traced here: 50.4 us
  Pallas kernels  49.8 us (98%)
  between operations  0.64 us (1%)
    pallas_call x1, Pallas kernels, body(): pl.pallas_call(functools.partial(kernel, sizes), out_shape=(jax.ShapeDtyp...  49 us

profile of v5, /device:TPU:1, one launch (start us, length us, event | category | flops | bytes accessed | tf_op | source)
XLA Modules:
  0.0 50.4 jit_solution(7446075863716724625)
XLA Ops:
  0.6 49.0 %shard_map.84 = (f32[4,32,512]{2,1,0:T(8,128)S(1)}, f32[1,512]{1,0:T(1,128)S(1)}, f32[1,512]{1,0:T(1,128)S(1)}, f32[9,512]{1,0:T(8,128)S(1)}) custom-call(f32[4,32,512]{2,1,0:T(8,128)} %q_hbm.1, f32[4,32,512]{2,1,0:T(8,128)} %c_hbm.1, f32[1,512]{1,0:T(1,128)} %k_hbm.1, f32[1,512]{1,0:T(1,128)} %v_hbm.1, f32[9,512]{1,0:T(8,128)} %t_hbm.1), custom_call_target="tpu_custom_call" | custom-call | tf_op jit(solution)/shard_map/pallas_call | solution.py:563
  49.7 0.7 %shard_map.85 = (f32[4,32,512]{2,1,0:T(8,128)}, f32[1,512]{1,0:T(1,128)}, f32[1,512]{1,0:T(1,128)}, f32[9,512]{1,0:T(8,128)}) custom-call(f32[4,32,512]{2,1,0:T(8,128)S(1)} %get-tuple-element.8.refs_0_, f32[1,512]{1,0:T(1,128)S(1)} %get-tuple-element.9.refs_1_, f32[1,512]{1,0:T(1,128)S(1)} %get-tuple-element.10.refs_2_, f32[9,512]{1,0:T(8,128)S(1)} %get-tuple-element.11.refs_3_), custom_call_target="tpu_custom_call" | custom-call | tf_op jit(solution)/shard_map/pallas_call | solution.py:491
